TPU v7x, 512 devices: a whole 4x4x16 slice. The times are simulated.
512 devices in a mesh: ctx: 16 (over z_lo, core), head: 8 (over x, z_hi), dp: 4 (over y).
Axes of the slice: x: 4, y: 4, z: 16 (z_hi: 2, z_lo: 8; z = z_hi * 8 + z_lo), core: 2. Of those that a mesh axis runs over, the one named last changes fastest.
Arguments:
- queries: bfloat16 [8192, 4096], P(('dp', 'ctx'), 'head'), parts along dimension 0, may hold values from -6 to 6
- key_rows: bfloat16 [8192, 4096], P(('dp', 'ctx'), 'head'), parts along dimension 0, may hold values from -6 to 6
- value_rows: bfloat16 [8192, 4096], P(('dp', 'ctx'), 'head'), parts along dimension 0, may hold values from -6 to 6
- gate_values: bfloat16 [8192, 4096], P(('dp', 'ctx'), 'head'), parts along dimension 0, may hold values from -6 to 6
- cotangent: bfloat16 [8192, 4096], P(('dp', 'ctx'), 'head'), parts along dimension 0, may hold values from -6 to 6
- decay_rates: float32 [16, 4096], P(None, 'head'), may hold values from 0 to 1, as said below
- residues: float32 [16, 4096], P(None, 'head'), may hold values from -4 to 4
- skip_gain: float32 [4096], P('head'), may hold values from -6 to 6
Outputs:
- queries_adjoint: bfloat16 [8192, 4096], P(('dp', 'ctx'), 'head'), parts along dimension 0
- keys_adjoint: bfloat16 [8192, 4096], P(('dp', 'ctx'), 'head'), parts along dimension 0
- values_adjoint: bfloat16 [8192, 4096], P(('dp', 'ctx'), 'head'), parts along dimension 0
- gate_adjoint: bfloat16 [8192, 4096], P(('dp', 'ctx'), 'head'), parts along dimension 0
- residues_adjoint: float32 [64, 4096], P('dp', 'head'), parts along dimension 0
There are 4 independent parts, one for each index of `dp`. A program takes and returns all parts, laid end to end along the dimension named above; an argument that names none is the same for every part. Nothing has to cross between parts.
Inputs may be any that keep to these rules, and one draw needn't show every extreme that they name: `decay_rates`: every rate lies between 0.6 / 2048 and 1/16 per position.
All inputs are finite; a program needn't handle non-finite values.
Results may differ from a plain program's by a relative error of at most 0.0094.
Values may be sent and summed in bfloat16 or wider, within the bound.
No kernel may reach another device: no remote copies, remote signals or barrier semaphores. Data moves between devices by JAX's collectives and lax.ppermute only.
A program may use at most 64 MiB of HBM per device.

v0:
```python
import math
import jax
import jax.numpy as jnp
from jax import lax
from jax.sharding import PartitionSpec as P

HEAD = 128
WIN = 4


def passed_along(array, axis, by):
    length = lax.axis_size(axis)
    return lax.ppermute(array, axis, [(i, (i + by) % length) for i in range(length)])


def window_mask(row_count):
    row_ids = jnp.arange(row_count)[:, None, None]
    lag_ids = jnp.arange(WIN + 1)[None, :, None]
    column_ids = jnp.arange(row_count)[None, None, :]
    return ((lag_ids > 0) | (column_ids <= row_ids)) & ((lag_ids < WIN) | (column_ids > row_ids))


def local(queries, key_rows, value_rows, gate_values, cotangent, decay_rates, residues, skip_gain):
    members = lax.axis_size("ctx")
    tok_rows, channels = queries.shape
    local_heads = channels // HEAD
    scale_factor = 1.0 / math.sqrt(HEAD)
    weights = jnp.sqrt(-jnp.expm1(-2.0 * decay_rates))
    mixing = residues * weights
    loop_gap = -jnp.expm1(-decay_rates * (tok_rows * members))
    device_decay = jnp.exp(-decay_rates * tok_rows)
    piece_rows = min(128, tok_rows)
    pieces = tok_rows // piece_rows
    offsets = jnp.arange(piece_rows, dtype=jnp.float32)[:, None, None]
    piece_index = jnp.arange(pieces, dtype=jnp.float32)[:, None, None]
    start_weights = jnp.exp(-decay_rates[None] * offsets)
    growth = jnp.exp(decay_rates[None] * offsets)
    delta_rows = cotangent.astype(jnp.float32) * gate_values.astype(jnp.float32)
    blocks_delta = delta_rows.reshape(pieces, piece_rows, channels)
    piece_starts = jnp.einsum(
        "qpc,mqc->mpc", start_weights, blocks_delta, precision=lax.Precision.HIGHEST
    )
    head_state = jnp.sum(
        jnp.exp(-decay_rates[None] * (piece_index * piece_rows)) * piece_starts, axis=0
    )

    def backward_turn(turn_index, moving):
        return passed_along(device_decay * moving + head_state, "ctx", -1)

    incoming = lax.fori_loop(0, members, backward_turn, jnp.zeros_like(head_state)) / loop_gap

    def backward_step(carried, segment):
        local_part = growth * lax.cumsum(start_weights * segment[:, None, :], axis=0, reverse=True)
        states = local_part + jnp.exp(-decay_rates[None] * (piece_rows - offsets)) * carried[None]
        mixture = jnp.sum(mixing[None] * states, axis=1) + skip_gain[None] * segment
        return (states[0], mixture)

    unused_state, adjoint_rows = lax.scan(backward_step, incoming, blocks_delta, reverse=True)
    attended_adjoint = adjoint_rows.reshape(tok_rows, channels).astype(jnp.bfloat16)
    key_value = jnp.stack([key_rows, value_rows])
    window = [key_value]
    moving = key_value
    for lag_index in range(WIN):
        moving = passed_along(moving, "ctx", 1)
        window.append(moving)
    stacked = jnp.stack(window)
    key_window = stacked[:, 0]
    value_window = stacked[:, 1]
    allowed = window_mask(tok_rows)
    attended_parts = []
    query_adjoints = []
    key_partials = []
    value_partials = []
    for head_index in range(local_heads):
        first = head_index * HEAD
        query_head = queries[:, first : first + HEAD]
        key_head = key_window[:, :, first : first + HEAD]
        value_head = value_window[:, :, first : first + HEAD]
        adjoint_head = attended_adjoint[:, first : first + HEAD]
        scores = (
            jnp.einsum("re,kse->rks", query_head, key_head, preferred_element_type=jnp.float32)
            * scale_factor
        )
        masked = jnp.where(allowed, scores, -jnp.inf)
        row_top = jnp.max(masked, axis=(1, 2), keepdims=True)
        raised = jnp.exp(masked - row_top)
        probability = raised / jnp.sum(raised, axis=(1, 2), keepdims=True)
        rounded_prob = probability.astype(jnp.bfloat16)
        attended_parts.append(
            jnp.einsum(
                "rks,kse->re", rounded_prob, value_head, preferred_element_type=jnp.float32
            ).astype(jnp.bfloat16)
        )
        weight_adjoint = jnp.einsum(
            "re,kse->rks", adjoint_head, value_head, preferred_element_type=jnp.float32
        )
        inner_sum = jnp.sum(probability * weight_adjoint, axis=(1, 2), keepdims=True)
        score_adjoint = (probability * (weight_adjoint - inner_sum) * scale_factor).astype(
            jnp.bfloat16
        )
        query_adjoints.append(
            jnp.einsum(
                "rks,kse->re", score_adjoint, key_head, preferred_element_type=jnp.float32
            ).astype(jnp.bfloat16)
        )
        key_partials.append(
            jnp.einsum(
                "rks,re->kse", score_adjoint, query_head, preferred_element_type=jnp.float32
            ).astype(jnp.bfloat16)
        )
        value_partials.append(
            jnp.einsum(
                "rks,re->kse", rounded_prob, adjoint_head, preferred_element_type=jnp.float32
            ).astype(jnp.bfloat16)
        )
    attended = jnp.concatenate(attended_parts, axis=1)
    queries_adjoint = jnp.concatenate(query_adjoints, axis=1)
    partials = jnp.stack(
        [jnp.concatenate(key_partials, axis=2), jnp.concatenate(value_partials, axis=2)], axis=1
    )
    collected = partials[0].astype(jnp.float32)
    for lag_index in range(1, WIN + 1):
        collected = collected + passed_along(partials[lag_index], "ctx", -lag_index).astype(
            jnp.float32
        )
    keys_adjoint = collected[0].astype(jnp.bfloat16)
    values_adjoint = collected[1].astype(jnp.bfloat16)
    signal = attended.astype(jnp.float32)
    blocks_signal = signal.reshape(pieces, piece_rows, channels)
    end_weights = jnp.exp(-decay_rates[None] * (piece_rows - 1.0 - offsets))
    piece_ends = jnp.einsum(
        "qpc,mqc->mpc", end_weights, blocks_signal, precision=lax.Precision.HIGHEST
    )
    tail_state = jnp.sum(
        jnp.exp(-decay_rates[None] * ((pieces - 1.0 - piece_index) * piece_rows)) * piece_ends,
        axis=0,
    )

    def forward_turn(turn_index, moving):
        return passed_along(device_decay * moving + tail_state, "ctx", 1)

    arriving = lax.fori_loop(0, members, forward_turn, jnp.zeros_like(tail_state)) / loop_gap
    entering = jnp.exp(-decay_rates[None] * (offsets + 1.0))

    def forward_step(carried, step_item):
        segment, matched = step_item
        local_part = start_weights * jnp.cumsum(growth * segment[:, None, :], axis=0)
        states = local_part + entering * carried[None]
        mixture = jnp.sum(mixing[None] * states, axis=1) + skip_gain[None] * segment
        product = jnp.sum(weights[None] * matched[:, None, :] * states, axis=0)
        return (states[-1], (mixture, product))

    closing, (mixed_rows, products) = lax.scan(
        forward_step, arriving, (blocks_signal, blocks_delta)
    )
    gate_adjoint = (cotangent.astype(jnp.float32) * mixed_rows.reshape(tok_rows, channels)).astype(
        jnp.bfloat16
    )
    residues_adjoint = lax.psum(jnp.sum(products, axis=0), "ctx")
    return (queries_adjoint, keys_adjoint, values_adjoint, gate_adjoint, residues_adjoint)


def solution(mesh):
    in_specs = (
        P(("dp", "ctx"), "head"),
        P(("dp", "ctx"), "head"),
        P(("dp", "ctx"), "head"),
        P(("dp", "ctx"), "head"),
        P(("dp", "ctx"), "head"),
        P(None, "head"),
        P(None, "head"),
        P("head"),
    )
    out_specs = (
        P(("dp", "ctx"), "head"),
        P(("dp", "ctx"), "head"),
        P(("dp", "ctx"), "head"),
        P(("dp", "ctx"), "head"),
        P("dp", "head"),
    )
    return jax.shard_map(local, mesh=mesh, in_specs=in_specs, out_specs=out_specs, check_vma=False)
```

profile of v0, /device:TPU:30, one launch (start us, length us, event | category | flops | bytes accessed | tf_op | source)
XLA Modules:
  0.0 588.1 jit_solution(3463437683806566200)
XLA Ops:
  1.7 1.9 collective-permute-start.2
  5.4 11.1 %fusion.2 = f32[128,16,512]{2,1,0:T(8,128)} fusion(f32[128,512]{1,0:T(8,128)S(1)} %get-tuple-element.151, f32[16,512]{1,0:T(8,128)S(1)} %get-tuple-element.163), kind=kOutput, calls=%fused_computation.10 | output fusion | flops 135266304 | bytes 4489216 | tf_op jit(solution)/shard_map/while/body/eval_jaxpr/reduce_window_sum | solution.py:53
  18.3 2.2 collective-permute-start.3
  21.2 12.1 %collective-permute-done.3 = bf16[2,128,512]{2,1,0:T(8,128)(2,1)S(1)} collective-permute-done((bf16[2,128,512]{2,1,0:T(8,128)(2,1)S(1)}, bf16[2,128,512]{2,1,0:T(8,128)(2,1)S(1)}, u32[]{:S(2)}, u32[]{:S(2)}) %collective-permute-start.3) | collective-permute-done | bytes 262176 | tf_op jit(solution)/shard_map/ppermute | solution.py:13
  33.2 1.9 collective-permute-start.4
  35.7 11.8 %collective-permute-done.4 = bf16[2,128,512]{2,1,0:T(8,128)(2,1)S(1)} collective-permute-done((bf16[2,128,512]{2,1,0:T(8,128)(2,1)S(1)}, bf16[2,128,512]{2,1,0:T(8,128)(2,1)S(1)}, u32[]{:S(2)}, u32[]{:S(2)}) %collective-permute-start.4) | collective-permute-done | bytes 262176 | tf_op jit(solution)/shard_map/ppermute | solution.py:13
  47.5 2.1 collective-permute-start.5
  49.7 12.6 %collective-permute-done.5 = bf16[2,128,512]{2,1,0:T(8,128)(2,1)S(1)} collective-permute-done((bf16[2,128,512]{2,1,0:T(8,128)(2,1)S(1)}, bf16[2,128,512]{2,1,0:T(8,128)(2,1)S(1)}, u32[]{:S(2)}, u32[]{:S(2)}) %collective-permute-start.5) | collective-permute-done | bytes 262176 | tf_op jit(solution)/shard_map/ppermute | solution.py:13
  68.1 181.3 %while.4 = (s32[]{:T(128)}, f32[16,512]{1,0:T(8,128)S(1)}, f32[16,512]{1,0:T(8,128)S(1)}, f32[16,512]{1,0:T(8,128)S(1)}, s32[]{:T(128)}) while((s32[]{:T(128)}, f32[16,512]{1,0:T(8,128)S(1)}, f32[16,512]{1,0:T(8,128)S(1)}, f32[16,512]{1,0:T(8,128)S(1)}, s32[]{:T(128)}) %tuple.67), condition=%wide.region_4.0_spmd, body=%wide.region_3.4_spmd.sunk | while | flops 16386 | bytes 262245 | solution.py:50
  68.1 1.9 collective-permute-start
  71.6 10.3 %collective-permute-start = (f32[16,512]{1,0:T(8,128)S(1)}, f32[16,512]{1,0:T(8,128)S(1)}, u32[]{:S(2)}, u32[]{:S(2)}) collective-permute-start(f32[16,512]{1,0:T(8,128)S(1)} %multiply_add_fusion.5), channel_id=1, source_target_pairs={{0,480},{32,0},{64,32},{96,64},{128,96},{160,128},{192,160},{224,1... | collective-permute-start | bytes 98312 | tf_op jit(solution)/shard_map/while/body/eval_jaxpr/ppermute | solution.py:13
  83.5 10.3 %collective-permute-start = (f32[16,512]{1,0:T(8,128)S(1)}, f32[16,512]{1,0:T(8,128)S(1)}, u32[]{:S(2)}, u32[]{:S(2)}) collective-permute-start(f32[16,512]{1,0:T(8,128)S(1)} %multiply_add_fusion.5), channel_id=1, source_target_pairs={{0,480},{32,0},{64,32},{96,64},{128,96},{160,128},{192,160},{224,1... | collective-permute-start | bytes 98312 | tf_op jit(solution)/shard_map/while/body/eval_jaxpr/ppermute | solution.py:13
  95.3 10.3 %collective-permute-start = (f32[16,512]{1,0:T(8,128)S(1)}, f32[16,512]{1,0:T(8,128)S(1)}, u32[]{:S(2)}, u32[]{:S(2)}) collective-permute-start(f32[16,512]{1,0:T(8,128)S(1)} %multiply_add_fusion.5), channel_id=1, source_target_pairs={{0,480},{32,0},{64,32},{96,64},{128,96},{160,128},{192,160},{224,1... | collective-permute-start | bytes 98312 | tf_op jit(solution)/shard_map/while/body/eval_jaxpr/ppermute | solution.py:13
  107.2 10.3 %collective-permute-start = (f32[16,512]{1,0:T(8,128)S(1)}, f32[16,512]{1,0:T(8,128)S(1)}, u32[]{:S(2)}, u32[]{:S(2)}) collective-permute-start(f32[16,512]{1,0:T(8,128)S(1)} %multiply_add_fusion.5), channel_id=1, source_target_pairs={{0,480},{32,0},{64,32},{96,64},{128,96},{160,128},{192,160},{224,1... | collective-permute-start | bytes 98312 | tf_op jit(solution)/shard_map/while/body/eval_jaxpr/ppermute | solution.py:13
  119.0 10.3 %collective-permute-start = (f32[16,512]{1,0:T(8,128)S(1)}, f32[16,512]{1,0:T(8,128)S(1)}, u32[]{:S(2)}, u32[]{:S(2)}) collective-permute-start(f32[16,512]{1,0:T(8,128)S(1)} %multiply_add_fusion.5), channel_id=1, source_target_pairs={{0,480},{32,0},{64,32},{96,64},{128,96},{160,128},{192,160},{224,1... | collective-permute-start | bytes 98312 | tf_op jit(solution)/shard_map/while/body/eval_jaxpr/ppermute | solution.py:13
  130.9 10.3 %collective-permute-start = (f32[16,512]{1,0:T(8,128)S(1)}, f32[16,512]{1,0:T(8,128)S(1)}, u32[]{:S(2)}, u32[]{:S(2)}) collective-permute-start(f32[16,512]{1,0:T(8,128)S(1)} %multiply_add_fusion.5), channel_id=1, source_target_pairs={{0,480},{32,0},{64,32},{96,64},{128,96},{160,128},{192,160},{224,1... | collective-permute-start | bytes 98312 | tf_op jit(solution)/shard_map/while/body/eval_jaxpr/ppermute | solution.py:13
  142.7 10.3 %collective-permute-start = (f32[16,512]{1,0:T(8,128)S(1)}, f32[16,512]{1,0:T(8,128)S(1)}, u32[]{:S(2)}, u32[]{:S(2)}) collective-permute-start(f32[16,512]{1,0:T(8,128)S(1)} %multiply_add_fusion.5), channel_id=1, source_target_pairs={{0,480},{32,0},{64,32},{96,64},{128,96},{160,128},{192,160},{224,1... | collective-permute-start | bytes 98312 | tf_op jit(solution)/shard_map/while/body/eval_jaxpr/ppermute | solution.py:13
  154.6 10.3 %collective-permute-start = (f32[16,512]{1,0:T(8,128)S(1)}, f32[16,512]{1,0:T(8,128)S(1)}, u32[]{:S(2)}, u32[]{:S(2)}) collective-permute-start(f32[16,512]{1,0:T(8,128)S(1)} %multiply_add_fusion.5), channel_id=1, source_target_pairs={{0,480},{32,0},{64,32},{96,64},{128,96},{160,128},{192,160},{224,1... | collective-permute-start | bytes 98312 | tf_op jit(solution)/shard_map/while/body/eval_jaxpr/ppermute | solution.py:13
  166.4 10.3 %collective-permute-start = (f32[16,512]{1,0:T(8,128)S(1)}, f32[16,512]{1,0:T(8,128)S(1)}, u32[]{:S(2)}, u32[]{:S(2)}) collective-permute-start(f32[16,512]{1,0:T(8,128)S(1)} %multiply_add_fusion.5), channel_id=1, source_target_pairs={{0,480},{32,0},{64,32},{96,64},{128,96},{160,128},{192,160},{224,1... | collective-permute-start | bytes 98312 | tf_op jit(solution)/shard_map/while/body/eval_jaxpr/ppermute | solution.py:13
  178.3 10.3 %collective-permute-start = (f32[16,512]{1,0:T(8,128)S(1)}, f32[16,512]{1,0:T(8,128)S(1)}, u32[]{:S(2)}, u32[]{:S(2)}) collective-permute-start(f32[16,512]{1,0:T(8,128)S(1)} %multiply_add_fusion.5), channel_id=1, source_target_pairs={{0,480},{32,0},{64,32},{96,64},{128,96},{160,128},{192,160},{224,1... | collective-permute-start | bytes 98312 | tf_op jit(solution)/shard_map/while/body/eval_jaxpr/ppermute | solution.py:13
  190.1 10.3 %collective-permute-start = (f32[16,512]{1,0:T(8,128)S(1)}, f32[16,512]{1,0:T(8,128)S(1)}, u32[]{:S(2)}, u32[]{:S(2)}) collective-permute-start(f32[16,512]{1,0:T(8,128)S(1)} %multiply_add_fusion.5), channel_id=1, source_target_pairs={{0,480},{32,0},{64,32},{96,64},{128,96},{160,128},{192,160},{224,1... | collective-permute-start | bytes 98312 | tf_op jit(solution)/shard_map/while/body/eval_jaxpr/ppermute | solution.py:13
  202.0 10.3 %collective-permute-start = (f32[16,512]{1,0:T(8,128)S(1)}, f32[16,512]{1,0:T(8,128)S(1)}, u32[]{:S(2)}, u32[]{:S(2)}) collective-permute-start(f32[16,512]{1,0:T(8,128)S(1)} %multiply_add_fusion.5), channel_id=1, source_target_pairs={{0,480},{32,0},{64,32},{96,64},{128,96},{160,128},{192,160},{224,1... | collective-permute-start | bytes 98312 | tf_op jit(solution)/shard_map/while/body/eval_jaxpr/ppermute | solution.py:13
  213.9 10.3 %collective-permute-start = (f32[16,512]{1,0:T(8,128)S(1)}, f32[16,512]{1,0:T(8,128)S(1)}, u32[]{:S(2)}, u32[]{:S(2)}) collective-permute-start(f32[16,512]{1,0:T(8,128)S(1)} %multiply_add_fusion.5), channel_id=1, source_target_pairs={{0,480},{32,0},{64,32},{96,64},{128,96},{160,128},{192,160},{224,1... | collective-permute-start | bytes 98312 | tf_op jit(solution)/shard_map/while/body/eval_jaxpr/ppermute | solution.py:13
  225.7 10.3 %collective-permute-start = (f32[16,512]{1,0:T(8,128)S(1)}, f32[16,512]{1,0:T(8,128)S(1)}, u32[]{:S(2)}, u32[]{:S(2)}) collective-permute-start(f32[16,512]{1,0:T(8,128)S(1)} %multiply_add_fusion.5), channel_id=1, source_target_pairs={{0,480},{32,0},{64,32},{96,64},{128,96},{160,128},{192,160},{224,1... | collective-permute-start | bytes 98312 | tf_op jit(solution)/shard_map/while/body/eval_jaxpr/ppermute | solution.py:13
  237.6 10.3 %collective-permute-start = (f32[16,512]{1,0:T(8,128)S(1)}, f32[16,512]{1,0:T(8,128)S(1)}, u32[]{:S(2)}, u32[]{:S(2)}) collective-permute-start(f32[16,512]{1,0:T(8,128)S(1)} %multiply_add_fusion.5), channel_id=1, source_target_pairs={{0,480},{32,0},{64,32},{96,64},{128,96},{160,128},{192,160},{224,1... | collective-permute-start | bytes 98312 | tf_op jit(solution)/shard_map/while/body/eval_jaxpr/ppermute | solution.py:13
  249.4 189.8 %while.5 = (s32[]{:T(128)}, f32[16,512]{1,0:T(8,128)S(1)}, f32[16,512]{1,0:T(8,128)S(1)}, f32[16,512]{1,0:T(8,128)S(1)}, s32[]{:T(128)}) while((s32[]{:T(128)}, f32[16,512]{1,0:T(8,128)S(1)}, f32[16,512]{1,0:T(8,128)S(1)}, f32[16,512]{1,0:T(8,128)S(1)}, s32[]{:T(128)}) %tuple.73), condition=%wide.region_18.19_spmd, body=%wide.region_17.18_spmd.sunk | while | flops 16386 | bytes 262245 | solution.py:142
  249.4 1.9 collective-permute-start.1
  251.3 9.9 %collective-permute-done.1 = f32[16,512]{1,0:T(8,128)S(1)} collective-permute-done((f32[16,512]{1,0:T(8,128)S(1)}, f32[16,512]{1,0:T(8,128)S(1)}, u32[]{:S(2)}, u32[]{:S(2)}) %collective-permute-start.1) | collective-permute-done | bytes 32800 | tf_op jit(solution)/shard_map/while/body/eval_jaxpr/ppermute | solution.py:13
  261.3 1.9 collective-permute-start.1
  263.2 9.9 %collective-permute-done.1 = f32[16,512]{1,0:T(8,128)S(1)} collective-permute-done((f32[16,512]{1,0:T(8,128)S(1)}, f32[16,512]{1,0:T(8,128)S(1)}, u32[]{:S(2)}, u32[]{:S(2)}) %collective-permute-start.1) | collective-permute-done | bytes 32800 | tf_op jit(solution)/shard_map/while/body/eval_jaxpr/ppermute | solution.py:13
  273.1 1.9 collective-permute-start.1
  275.0 9.9 %collective-permute-done.1 = f32[16,512]{1,0:T(8,128)S(1)} collective-permute-done((f32[16,512]{1,0:T(8,128)S(1)}, f32[16,512]{1,0:T(8,128)S(1)}, u32[]{:S(2)}, u32[]{:S(2)}) %collective-permute-start.1) | collective-permute-done | bytes 32800 | tf_op jit(solution)/shard_map/while/body/eval_jaxpr/ppermute | solution.py:13
  285.0 1.9 collective-permute-start.1
  286.9 9.9 %collective-permute-done.1 = f32[16,512]{1,0:T(8,128)S(1)} collective-permute-done((f32[16,512]{1,0:T(8,128)S(1)}, f32[16,512]{1,0:T(8,128)S(1)}, u32[]{:S(2)}, u32[]{:S(2)}) %collective-permute-start.1) | collective-permute-done | bytes 32800 | tf_op jit(solution)/shard_map/while/body/eval_jaxpr/ppermute | solution.py:13
  296.8 1.9 collective-permute-start.1
  298.7 9.9 %collective-permute-done.1 = f32[16,512]{1,0:T(8,128)S(1)} collective-permute-done((f32[16,512]{1,0:T(8,128)S(1)}, f32[16,512]{1,0:T(8,128)S(1)}, u32[]{:S(2)}, u32[]{:S(2)}) %collective-permute-start.1) | collective-permute-done | bytes 32800 | tf_op jit(solution)/shard_map/while/body/eval_jaxpr/ppermute | solution.py:13
  308.7 1.9 collective-permute-start.1
  310.6 9.9 %collective-permute-done.1 = f32[16,512]{1,0:T(8,128)S(1)} collective-permute-done((f32[16,512]{1,0:T(8,128)S(1)}, f32[16,512]{1,0:T(8,128)S(1)}, u32[]{:S(2)}, u32[]{:S(2)}) %collective-permute-start.1) | collective-permute-done | bytes 32800 | tf_op jit(solution)/shard_map/while/body/eval_jaxpr/ppermute | solution.py:13
  320.5 1.9 collective-permute-start.1
  322.5 9.9 %collective-permute-done.1 = f32[16,512]{1,0:T(8,128)S(1)} collective-permute-done((f32[16,512]{1,0:T(8,128)S(1)}, f32[16,512]{1,0:T(8,128)S(1)}, u32[]{:S(2)}, u32[]{:S(2)}) %collective-permute-start.1) | collective-permute-done | bytes 32800 | tf_op jit(solution)/shard_map/while/body/eval_jaxpr/ppermute | solution.py:13
  332.4 1.9 collective-permute-start.1
  334.3 9.9 %collective-permute-done.1 = f32[16,512]{1,0:T(8,128)S(1)} collective-permute-done((f32[16,512]{1,0:T(8,128)S(1)}, f32[16,512]{1,0:T(8,128)S(1)}, u32[]{:S(2)}, u32[]{:S(2)}) %collective-permute-start.1) | collective-permute-done | bytes 32800 | tf_op jit(solution)/shard_map/while/body/eval_jaxpr/ppermute | solution.py:13
  344.2 1.9 collective-permute-start.1
  346.2 9.9 %collective-permute-done.1 = f32[16,512]{1,0:T(8,128)S(1)} collective-permute-done((f32[16,512]{1,0:T(8,128)S(1)}, f32[16,512]{1,0:T(8,128)S(1)}, u32[]{:S(2)}, u32[]{:S(2)}) %collective-permute-start.1) | collective-permute-done | bytes 32800 | tf_op jit(solution)/shard_map/while/body/eval_jaxpr/ppermute | solution.py:13
  356.1 1.9 collective-permute-start.1
  358.0 9.9 %collective-permute-done.1 = f32[16,512]{1,0:T(8,128)S(1)} collective-permute-done((f32[16,512]{1,0:T(8,128)S(1)}, f32[16,512]{1,0:T(8,128)S(1)}, u32[]{:S(2)}, u32[]{:S(2)}) %collective-permute-start.1) | collective-permute-done | bytes 32800 | tf_op jit(solution)/shard_map/while/body/eval_jaxpr/ppermute | solution.py:13
  367.9 1.9 collective-permute-start.1
  369.9 9.9 %collective-permute-done.1 = f32[16,512]{1,0:T(8,128)S(1)} collective-permute-done((f32[16,512]{1,0:T(8,128)S(1)}, f32[16,512]{1,0:T(8,128)S(1)}, u32[]{:S(2)}, u32[]{:S(2)}) %collective-permute-start.1) | collective-permute-done | bytes 32800 | tf_op jit(solution)/shard_map/while/body/eval_jaxpr/ppermute | solution.py:13
  379.8 1.9 collective-permute-start.1
  381.7 9.9 %collective-permute-done.1 = f32[16,512]{1,0:T(8,128)S(1)} collective-permute-done((f32[16,512]{1,0:T(8,128)S(1)}, f32[16,512]{1,0:T(8,128)S(1)}, u32[]{:S(2)}, u32[]{:S(2)}) %collective-permute-start.1) | collective-permute-done | bytes 32800 | tf_op jit(solution)/shard_map/while/body/eval_jaxpr/ppermute | solution.py:13
  391.6 1.9 collective-permute-start.1
  393.6 9.9 %collective-permute-done.1 = f32[16,512]{1,0:T(8,128)S(1)} collective-permute-done((f32[16,512]{1,0:T(8,128)S(1)}, f32[16,512]{1,0:T(8,128)S(1)}, u32[]{:S(2)}, u32[]{:S(2)}) %collective-permute-start.1) | collective-permute-done | bytes 32800 | tf_op jit(solution)/shard_map/while/body/eval_jaxpr/ppermute | solution.py:13
  403.5 1.9 collective-permute-start.1
  405.4 9.9 %collective-permute-done.1 = f32[16,512]{1,0:T(8,128)S(1)} collective-permute-done((f32[16,512]{1,0:T(8,128)S(1)}, f32[16,512]{1,0:T(8,128)S(1)}, u32[]{:S(2)}, u32[]{:S(2)}) %collective-permute-start.1) | collective-permute-done | bytes 32800 | tf_op jit(solution)/shard_map/while/body/eval_jaxpr/ppermute | solution.py:13
  415.3 1.9 collective-permute-start.1
  417.3 10.0 %collective-permute-done.1 = f32[16,512]{1,0:T(8,128)S(1)} collective-permute-done((f32[16,512]{1,0:T(8,128)S(1)}, f32[16,512]{1,0:T(8,128)S(1)}, u32[]{:S(2)}, u32[]{:S(2)}) %collective-permute-start.1) | collective-permute-done | bytes 32800 | tf_op jit(solution)/shard_map/while/body/eval_jaxpr/ppermute | solution.py:13
  427.3 1.9 collective-permute-start.1
  429.2 10.0 %collective-permute-done.1 = f32[16,512]{1,0:T(8,128)S(1)} collective-permute-done((f32[16,512]{1,0:T(8,128)S(1)}, f32[16,512]{1,0:T(8,128)S(1)}, u32[]{:S(2)}, u32[]{:S(2)}) %collective-permute-start.1) | collective-permute-done | bytes 32800 | tf_op jit(solution)/shard_map/while/body/eval_jaxpr/ppermute | solution.py:13
  439.4 29.8 %multiply_reduce_fusion.2 = (f32[16,512]{1,0:T(8,128)S(1)}, f32[128,512]{1,0:T(8,128)S(1)}, f32[128,512]{1,0:T(8,128)S(1)}) fusion(f32[16,512]{1,0:T(8,128)S(1)} %get-tuple-element.160, f32[128,512]{1,0:T(8,128)S(1)} %get-tuple-element.151, f32[16,512]{1,0:T(8,128)S(1)} %get-tuple-element.159, f32[16,512]{1,0:T(8,128)S(1)} %get-tuple-element.157, ...), kind=kOutput, calls=%fused_computation.4 | output fusion | flops 152952832 | bytes 5473280 | tf_op jit(solution)/shard_map/while/body/eval_jaxpr/jit(cumsum)/reduce_window_sum | solution.py:147
  475.2 1.9 collective-permute-start.6
  477.2 1.9 collective-permute-start.7
  479.1 1.9 collective-permute-start.9
  481.0 1.9 collective-permute-start.8
  484.0 101.4 %psum.7 = f32[16,512]{1,0:T(8,128)} all-reduce(f32[16,512]{1,0:T(8,128)S(1)} %get-tuple-element.122), channel_id=1, replica_groups=mesh['ctx'=16,'head'=8,'dp'=4] {'ctx'}, use_global_device_ids=true, to_apply=%region_21.22 | all-reduce | flops 8192 | bytes 65536 | tf_op jit(solution)/shard_map/psum | solution.py:159
  (150 shorter events, 46.7 us)
Async XLA Ops:
  0.6 20.5 %copy-start.2 = (bf16[128,512]{1,0:T(8,128)(2,1)S(1)}, bf16[128,512]{1,0:T(8,128)(2,1)}, u32[]{:S(2)}) copy-start(bf16[128,512]{1,0:T(8,128)(2,1)} %param.14) | copy-start | bytes 393220
  0.6 20.5 %copy-start.3 = (bf16[128,512]{1,0:T(8,128)(2,1)S(1)}, bf16[128,512]{1,0:T(8,128)(2,1)}, u32[]{:S(2)}) copy-start(bf16[128,512]{1,0:T(8,128)(2,1)} %param.13) | copy-start | bytes 393220
  1.7 16.6 %collective-permute-start.2 = (bf16[2,128,512]{2,1,0:T(8,128)(2,1)S(1)}, bf16[2,128,512]{2,1,0:T(8,128)(2,1)S(1)}, u32[]{:S(2)}, u32[]{:S(2)}) collective-permute-start(bf16[2,128,512]{2,1,0:T(8,128)(2,1)S(1)} %pad_maximum_fusion.1), channel_id=1, source_target_pairs={{0,32},{32,64},{64,96},{96,128},{128,160},{160,192},{192,224},{224... | collective-permute-start | bytes 786440 | tf_op jit(solution)/shard_map/ppermute | solution.py:13
  5.4 57.0 %copy-start.5 = (bf16[128,512]{1,0:T(8,128)(2,1)S(1)}, bf16[128,512]{1,0:T(8,128)(2,1)}, u32[]{:S(2)}) copy-start(bf16[128,512]{1,0:T(8,128)(2,1)} %param.12) | copy-start | bytes 393220
  18.3 14.9 %collective-permute-start.3 = (bf16[2,128,512]{2,1,0:T(8,128)(2,1)S(1)}, bf16[2,128,512]{2,1,0:T(8,128)(2,1)S(1)}, u32[]{:S(2)}, u32[]{:S(2)}) collective-permute-start(bf16[2,128,512]{2,1,0:T(8,128)(2,1)S(1)} %collective-permute-done.2), channel_id=1, source_target_pairs={{0,32},{32,64},{64,96},{96,128},{128,160},{160,192},{192,224},{224... | collective-permute-start | bytes 786440 | tf_op jit(solution)/shard_map/ppermute | solution.py:13
  33.2 14.3 %collective-permute-start.4 = (bf16[2,128,512]{2,1,0:T(8,128)(2,1)S(1)}, bf16[2,128,512]{2,1,0:T(8,128)(2,1)S(1)}, u32[]{:S(2)}, u32[]{:S(2)}) collective-permute-start(bf16[2,128,512]{2,1,0:T(8,128)(2,1)S(1)} %collective-permute-done.3), channel_id=1, source_target_pairs={{0,32},{32,64},{64,96},{96,128},{128,160},{160,192},{192,224},{224... | collective-permute-start | bytes 786440 | tf_op jit(solution)/shard_map/ppermute | solution.py:13
  47.5 14.8 %collective-permute-start.5 = (bf16[2,128,512]{2,1,0:T(8,128)(2,1)S(1)}, bf16[2,128,512]{2,1,0:T(8,128)(2,1)S(1)}, u32[]{:S(2)}, u32[]{:S(2)}) collective-permute-start(bf16[2,128,512]{2,1,0:T(8,128)(2,1)S(1)} %collective-permute-done.4), channel_id=1, source_target_pairs={{0,32},{32,64},{64,96},{96,128},{128,160},{160,192},{192,224},{224... | collective-permute-start | bytes 786440 | tf_op jit(solution)/shard_map/ppermute | solution.py:13
  62.7 1.8 copy-start.11
  63.5 2.8 copy-start.17
  63.6 0.5 copy-start.15
  64.2 3.8 copy-start.13
  64.5 3.6 copy-start.4
  64.6 0.6 copy-start.9
  64.9 374.3 %copy-start.7 = (f32[16,512]{1,0:T(8,128)S(1)}, f32[16,512]{1,0:T(8,128)}, u32[]{:S(2)}) copy-start(f32[16,512]{1,0:T(8,128)} %param.18) | copy-start | bytes 98308
  68.1 3.5 collective-permute-start
  71.6 11.8 %collective-permute-start = (f32[16,512]{1,0:T(8,128)S(1)}, f32[16,512]{1,0:T(8,128)S(1)}, u32[]{:S(2)}, u32[]{:S(2)}) collective-permute-start(f32[16,512]{1,0:T(8,128)S(1)} %multiply_add_fusion.5), channel_id=1, source_target_pairs={{0,480},{32,0},{64,32},{96,64},{128,96},{160,128},{192,160},{224,1... | collective-permute-start | bytes 98312 | tf_op jit(solution)/shard_map/while/body/eval_jaxpr/ppermute | solution.py:13
  83.5 11.8 %collective-permute-start = (f32[16,512]{1,0:T(8,128)S(1)}, f32[16,512]{1,0:T(8,128)S(1)}, u32[]{:S(2)}, u32[]{:S(2)}) collective-permute-start(f32[16,512]{1,0:T(8,128)S(1)} %multiply_add_fusion.5), channel_id=1, source_target_pairs={{0,480},{32,0},{64,32},{96,64},{128,96},{160,128},{192,160},{224,1... | collective-permute-start | bytes 98312 | tf_op jit(solution)/shard_map/while/body/eval_jaxpr/ppermute | solution.py:13
  95.3 11.8 %collective-permute-start = (f32[16,512]{1,0:T(8,128)S(1)}, f32[16,512]{1,0:T(8,128)S(1)}, u32[]{:S(2)}, u32[]{:S(2)}) collective-permute-start(f32[16,512]{1,0:T(8,128)S(1)} %multiply_add_fusion.5), channel_id=1, source_target_pairs={{0,480},{32,0},{64,32},{96,64},{128,96},{160,128},{192,160},{224,1... | collective-permute-start | bytes 98312 | tf_op jit(solution)/shard_map/while/body/eval_jaxpr/ppermute | solution.py:13
  107.2 11.8 %collective-permute-start = (f32[16,512]{1,0:T(8,128)S(1)}, f32[16,512]{1,0:T(8,128)S(1)}, u32[]{:S(2)}, u32[]{:S(2)}) collective-permute-start(f32[16,512]{1,0:T(8,128)S(1)} %multiply_add_fusion.5), channel_id=1, source_target_pairs={{0,480},{32,0},{64,32},{96,64},{128,96},{160,128},{192,160},{224,1... | collective-permute-start | bytes 98312 | tf_op jit(solution)/shard_map/while/body/eval_jaxpr/ppermute | solution.py:13
  119.0 11.8 %collective-permute-start = (f32[16,512]{1,0:T(8,128)S(1)}, f32[16,512]{1,0:T(8,128)S(1)}, u32[]{:S(2)}, u32[]{:S(2)}) collective-permute-start(f32[16,512]{1,0:T(8,128)S(1)} %multiply_add_fusion.5), channel_id=1, source_target_pairs={{0,480},{32,0},{64,32},{96,64},{128,96},{160,128},{192,160},{224,1... | collective-permute-start | bytes 98312 | tf_op jit(solution)/shard_map/while/body/eval_jaxpr/ppermute | solution.py:13
  130.9 11.8 %collective-permute-start = (f32[16,512]{1,0:T(8,128)S(1)}, f32[16,512]{1,0:T(8,128)S(1)}, u32[]{:S(2)}, u32[]{:S(2)}) collective-permute-start(f32[16,512]{1,0:T(8,128)S(1)} %multiply_add_fusion.5), channel_id=1, source_target_pairs={{0,480},{32,0},{64,32},{96,64},{128,96},{160,128},{192,160},{224,1... | collective-permute-start | bytes 98312 | tf_op jit(solution)/shard_map/while/body/eval_jaxpr/ppermute | solution.py:13
  142.7 11.8 %collective-permute-start = (f32[16,512]{1,0:T(8,128)S(1)}, f32[16,512]{1,0:T(8,128)S(1)}, u32[]{:S(2)}, u32[]{:S(2)}) collective-permute-start(f32[16,512]{1,0:T(8,128)S(1)} %multiply_add_fusion.5), channel_id=1, source_target_pairs={{0,480},{32,0},{64,32},{96,64},{128,96},{160,128},{192,160},{224,1... | collective-permute-start | bytes 98312 | tf_op jit(solution)/shard_map/while/body/eval_jaxpr/ppermute | solution.py:13
  154.6 11.8 %collective-permute-start = (f32[16,512]{1,0:T(8,128)S(1)}, f32[16,512]{1,0:T(8,128)S(1)}, u32[]{:S(2)}, u32[]{:S(2)}) collective-permute-start(f32[16,512]{1,0:T(8,128)S(1)} %multiply_add_fusion.5), channel_id=1, source_target_pairs={{0,480},{32,0},{64,32},{96,64},{128,96},{160,128},{192,160},{224,1... | collective-permute-start | bytes 98312 | tf_op jit(solution)/shard_map/while/body/eval_jaxpr/ppermute | solution.py:13
  166.4 11.8 %collective-permute-start = (f32[16,512]{1,0:T(8,128)S(1)}, f32[16,512]{1,0:T(8,128)S(1)}, u32[]{:S(2)}, u32[]{:S(2)}) collective-permute-start(f32[16,512]{1,0:T(8,128)S(1)} %multiply_add_fusion.5), channel_id=1, source_target_pairs={{0,480},{32,0},{64,32},{96,64},{128,96},{160,128},{192,160},{224,1... | collective-permute-start | bytes 98312 | tf_op jit(solution)/shard_map/while/body/eval_jaxpr/ppermute | solution.py:13
  178.3 11.8 %collective-permute-start = (f32[16,512]{1,0:T(8,128)S(1)}, f32[16,512]{1,0:T(8,128)S(1)}, u32[]{:S(2)}, u32[]{:S(2)}) collective-permute-start(f32[16,512]{1,0:T(8,128)S(1)} %multiply_add_fusion.5), channel_id=1, source_target_pairs={{0,480},{32,0},{64,32},{96,64},{128,96},{160,128},{192,160},{224,1... | collective-permute-start | bytes 98312 | tf_op jit(solution)/shard_map/while/body/eval_jaxpr/ppermute | solution.py:13
  190.1 11.8 %collective-permute-start = (f32[16,512]{1,0:T(8,128)S(1)}, f32[16,512]{1,0:T(8,128)S(1)}, u32[]{:S(2)}, u32[]{:S(2)}) collective-permute-start(f32[16,512]{1,0:T(8,128)S(1)} %multiply_add_fusion.5), channel_id=1, source_target_pairs={{0,480},{32,0},{64,32},{96,64},{128,96},{160,128},{192,160},{224,1... | collective-permute-start | bytes 98312 | tf_op jit(solution)/shard_map/while/body/eval_jaxpr/ppermute | solution.py:13
  202.0 11.8 %collective-permute-start = (f32[16,512]{1,0:T(8,128)S(1)}, f32[16,512]{1,0:T(8,128)S(1)}, u32[]{:S(2)}, u32[]{:S(2)}) collective-permute-start(f32[16,512]{1,0:T(8,128)S(1)} %multiply_add_fusion.5), channel_id=1, source_target_pairs={{0,480},{32,0},{64,32},{96,64},{128,96},{160,128},{192,160},{224,1... | collective-permute-start | bytes 98312 | tf_op jit(solution)/shard_map/while/body/eval_jaxpr/ppermute | solution.py:13
  213.9 11.8 %collective-permute-start = (f32[16,512]{1,0:T(8,128)S(1)}, f32[16,512]{1,0:T(8,128)S(1)}, u32[]{:S(2)}, u32[]{:S(2)}) collective-permute-start(f32[16,512]{1,0:T(8,128)S(1)} %multiply_add_fusion.5), channel_id=1, source_target_pairs={{0,480},{32,0},{64,32},{96,64},{128,96},{160,128},{192,160},{224,1... | collective-permute-start | bytes 98312 | tf_op jit(solution)/shard_map/while/body/eval_jaxpr/ppermute | solution.py:13
  225.7 11.8 %collective-permute-start = (f32[16,512]{1,0:T(8,128)S(1)}, f32[16,512]{1,0:T(8,128)S(1)}, u32[]{:S(2)}, u32[]{:S(2)}) collective-permute-start(f32[16,512]{1,0:T(8,128)S(1)} %multiply_add_fusion.5), channel_id=1, source_target_pairs={{0,480},{32,0},{64,32},{96,64},{128,96},{160,128},{192,160},{224,1... | collective-permute-start | bytes 98312 | tf_op jit(solution)/shard_map/while/body/eval_jaxpr/ppermute | solution.py:13
  237.6 11.8 %collective-permute-start = (f32[16,512]{1,0:T(8,128)S(1)}, f32[16,512]{1,0:T(8,128)S(1)}, u32[]{:S(2)}, u32[]{:S(2)}) collective-permute-start(f32[16,512]{1,0:T(8,128)S(1)} %multiply_add_fusion.5), channel_id=1, source_target_pairs={{0,480},{32,0},{64,32},{96,64},{128,96},{160,128},{192,160},{224,1... | collective-permute-start | bytes 98312 | tf_op jit(solution)/shard_map/while/body/eval_jaxpr/ppermute | solution.py:13
  249.4 11.8 %collective-permute-start.1 = (f32[16,512]{1,0:T(8,128)S(1)}, f32[16,512]{1,0:T(8,128)S(1)}, u32[]{:S(2)}, u32[]{:S(2)}) collective-permute-start(f32[16,512]{1,0:T(8,128)S(1)} %multiply_add_fusion.6), channel_id=1, source_target_pairs={{0,32},{32,64},{64,96},{96,128},{128,160},{160,192},{192,224},{224... | collective-permute-start | bytes 98312 | tf_op jit(solution)/shard_map/while/body/eval_jaxpr/ppermute | solution.py:13
  261.3 11.8 %collective-permute-start.1 = (f32[16,512]{1,0:T(8,128)S(1)}, f32[16,512]{1,0:T(8,128)S(1)}, u32[]{:S(2)}, u32[]{:S(2)}) collective-permute-start(f32[16,512]{1,0:T(8,128)S(1)} %multiply_add_fusion.6), channel_id=1, source_target_pairs={{0,32},{32,64},{64,96},{96,128},{128,160},{160,192},{192,224},{224... | collective-permute-start | bytes 98312 | tf_op jit(solution)/shard_map/while/body/eval_jaxpr/ppermute | solution.py:13
  273.1 11.8 %collective-permute-start.1 = (f32[16,512]{1,0:T(8,128)S(1)}, f32[16,512]{1,0:T(8,128)S(1)}, u32[]{:S(2)}, u32[]{:S(2)}) collective-permute-start(f32[16,512]{1,0:T(8,128)S(1)} %multiply_add_fusion.6), channel_id=1, source_target_pairs={{0,32},{32,64},{64,96},{96,128},{128,160},{160,192},{192,224},{224... | collective-permute-start | bytes 98312 | tf_op jit(solution)/shard_map/while/body/eval_jaxpr/ppermute | solution.py:13
  285.0 11.8 %collective-permute-start.1 = (f32[16,512]{1,0:T(8,128)S(1)}, f32[16,512]{1,0:T(8,128)S(1)}, u32[]{:S(2)}, u32[]{:S(2)}) collective-permute-start(f32[16,512]{1,0:T(8,128)S(1)} %multiply_add_fusion.6), channel_id=1, source_target_pairs={{0,32},{32,64},{64,96},{96,128},{128,160},{160,192},{192,224},{224... | collective-permute-start | bytes 98312 | tf_op jit(solution)/shard_map/while/body/eval_jaxpr/ppermute | solution.py:13
  296.8 11.8 %collective-permute-start.1 = (f32[16,512]{1,0:T(8,128)S(1)}, f32[16,512]{1,0:T(8,128)S(1)}, u32[]{:S(2)}, u32[]{:S(2)}) collective-permute-start(f32[16,512]{1,0:T(8,128)S(1)} %multiply_add_fusion.6), channel_id=1, source_target_pairs={{0,32},{32,64},{64,96},{96,128},{128,160},{160,192},{192,224},{224... | collective-permute-start | bytes 98312 | tf_op jit(solution)/shard_map/while/body/eval_jaxpr/ppermute | solution.py:13
  308.7 11.8 %collective-permute-start.1 = (f32[16,512]{1,0:T(8,128)S(1)}, f32[16,512]{1,0:T(8,128)S(1)}, u32[]{:S(2)}, u32[]{:S(2)}) collective-permute-start(f32[16,512]{1,0:T(8,128)S(1)} %multiply_add_fusion.6), channel_id=1, source_target_pairs={{0,32},{32,64},{64,96},{96,128},{128,160},{160,192},{192,224},{224... | collective-permute-start | bytes 98312 | tf_op jit(solution)/shard_map/while/body/eval_jaxpr/ppermute | solution.py:13
  320.5 11.8 %collective-permute-start.1 = (f32[16,512]{1,0:T(8,128)S(1)}, f32[16,512]{1,0:T(8,128)S(1)}, u32[]{:S(2)}, u32[]{:S(2)}) collective-permute-start(f32[16,512]{1,0:T(8,128)S(1)} %multiply_add_fusion.6), channel_id=1, source_target_pairs={{0,32},{32,64},{64,96},{96,128},{128,160},{160,192},{192,224},{224... | collective-permute-start | bytes 98312 | tf_op jit(solution)/shard_map/while/body/eval_jaxpr/ppermute | solution.py:13
  332.4 11.8 %collective-permute-start.1 = (f32[16,512]{1,0:T(8,128)S(1)}, f32[16,512]{1,0:T(8,128)S(1)}, u32[]{:S(2)}, u32[]{:S(2)}) collective-permute-start(f32[16,512]{1,0:T(8,128)S(1)} %multiply_add_fusion.6), channel_id=1, source_target_pairs={{0,32},{32,64},{64,96},{96,128},{128,160},{160,192},{192,224},{224... | collective-permute-start | bytes 98312 | tf_op jit(solution)/shard_map/while/body/eval_jaxpr/ppermute | solution.py:13
  344.2 11.8 %collective-permute-start.1 = (f32[16,512]{1,0:T(8,128)S(1)}, f32[16,512]{1,0:T(8,128)S(1)}, u32[]{:S(2)}, u32[]{:S(2)}) collective-permute-start(f32[16,512]{1,0:T(8,128)S(1)} %multiply_add_fusion.6), channel_id=1, source_target_pairs={{0,32},{32,64},{64,96},{96,128},{128,160},{160,192},{192,224},{224... | collective-permute-start | bytes 98312 | tf_op jit(solution)/shard_map/while/body/eval_jaxpr/ppermute | solution.py:13
  356.1 11.8 %collective-permute-start.1 = (f32[16,512]{1,0:T(8,128)S(1)}, f32[16,512]{1,0:T(8,128)S(1)}, u32[]{:S(2)}, u32[]{:S(2)}) collective-permute-start(f32[16,512]{1,0:T(8,128)S(1)} %multiply_add_fusion.6), channel_id=1, source_target_pairs={{0,32},{32,64},{64,96},{96,128},{128,160},{160,192},{192,224},{224... | collective-permute-start | bytes 98312 | tf_op jit(solution)/shard_map/while/body/eval_jaxpr/ppermute | solution.py:13
  367.9 11.8 %collective-permute-start.1 = (f32[16,512]{1,0:T(8,128)S(1)}, f32[16,512]{1,0:T(8,128)S(1)}, u32[]{:S(2)}, u32[]{:S(2)}) collective-permute-start(f32[16,512]{1,0:T(8,128)S(1)} %multiply_add_fusion.6), channel_id=1, source_target_pairs={{0,32},{32,64},{64,96},{96,128},{128,160},{160,192},{192,224},{224... | collective-permute-start | bytes 98312 | tf_op jit(solution)/shard_map/while/body/eval_jaxpr/ppermute | solution.py:13
  379.8 11.8 %collective-permute-start.1 = (f32[16,512]{1,0:T(8,128)S(1)}, f32[16,512]{1,0:T(8,128)S(1)}, u32[]{:S(2)}, u32[]{:S(2)}) collective-permute-start(f32[16,512]{1,0:T(8,128)S(1)} %multiply_add_fusion.6), channel_id=1, source_target_pairs={{0,32},{32,64},{64,96},{96,128},{128,160},{160,192},{192,224},{224... | collective-permute-start | bytes 98312 | tf_op jit(solution)/shard_map/while/body/eval_jaxpr/ppermute | solution.py:13
  391.6 11.8 %collective-permute-start.1 = (f32[16,512]{1,0:T(8,128)S(1)}, f32[16,512]{1,0:T(8,128)S(1)}, u32[]{:S(2)}, u32[]{:S(2)}) collective-permute-start(f32[16,512]{1,0:T(8,128)S(1)} %multiply_add_fusion.6), channel_id=1, source_target_pairs={{0,32},{32,64},{64,96},{96,128},{128,160},{160,192},{192,224},{224... | collective-permute-start | bytes 98312 | tf_op jit(solution)/shard_map/while/body/eval_jaxpr/ppermute | solution.py:13
  403.5 11.8 %collective-permute-start.1 = (f32[16,512]{1,0:T(8,128)S(1)}, f32[16,512]{1,0:T(8,128)S(1)}, u32[]{:S(2)}, u32[]{:S(2)}) collective-permute-start(f32[16,512]{1,0:T(8,128)S(1)} %multiply_add_fusion.6), channel_id=1, source_target_pairs={{0,32},{32,64},{64,96},{96,128},{128,160},{160,192},{192,224},{224... | collective-permute-start | bytes 98312 | tf_op jit(solution)/shard_map/while/body/eval_jaxpr/ppermute | solution.py:13
  415.3 11.9 %collective-permute-start.1 = (f32[16,512]{1,0:T(8,128)S(1)}, f32[16,512]{1,0:T(8,128)S(1)}, u32[]{:S(2)}, u32[]{:S(2)}) collective-permute-start(f32[16,512]{1,0:T(8,128)S(1)} %multiply_add_fusion.6), channel_id=1, source_target_pairs={{0,32},{32,64},{64,96},{96,128},{128,160},{160,192},{192,224},{224... | collective-permute-start | bytes 98312 | tf_op jit(solution)/shard_map/while/body/eval_jaxpr/ppermute | solution.py:13
  427.3 11.9 %collective-permute-start.1 = (f32[16,512]{1,0:T(8,128)S(1)}, f32[16,512]{1,0:T(8,128)S(1)}, u32[]{:S(2)}, u32[]{:S(2)}) collective-permute-start(f32[16,512]{1,0:T(8,128)S(1)} %multiply_add_fusion.6), channel_id=1, source_target_pairs={{0,32},{32,64},{64,96},{96,128},{128,160},{160,192},{192,224},{224... | collective-permute-start | bytes 98312 | tf_op jit(solution)/shard_map/while/body/eval_jaxpr/ppermute | solution.py:13
  439.3 29.9 %copy-start = (bf16[128,512]{1,0:T(8,128)(2,1)S(1)}, bf16[128,512]{1,0:T(8,128)(2,1)}, u32[]{:S(2)}) copy-start(bf16[128,512]{1,0:T(8,128)(2,1)} %param.16) | copy-start | bytes 393220
  439.3 29.9 %copy-start.1 = (bf16[128,512]{1,0:T(8,128)(2,1)S(1)}, bf16[128,512]{1,0:T(8,128)(2,1)}, u32[]{:S(2)}) copy-start(bf16[128,512]{1,0:T(8,128)(2,1)} %param.15) | copy-start | bytes 393220
  439.3 29.9 %copy-start.8 = (f32[512]{0:T(512)S(1)}, f32[512]{0:T(512)}, u32[]{:S(2)}) copy-start(f32[512]{0:T(512)} %param.19) | copy-start | bytes 6148
  439.3 30.6 %copy-start.12 = (f32[128]{0:T(128)S(1)}, f32[128]{0:T(128)}, u32[]{:S(2)}) copy-start(f32[128]{0:T(128)} %copy-done.11) | copy-start | bytes 1540
  439.3 30.6 %copy-start.16 = (f32[128]{0:T(128)S(1)}, f32[128]{0:T(128)}, u32[]{:S(2)}) copy-start(f32[128]{0:T(128)} %copy-done.15) | copy-start | bytes 1540
  439.3 30.8 %copy-start.14 = (f32[128]{0:T(128)S(1)}, f32[128]{0:T(128)}, u32[]{:S(2)}) copy-start(f32[128]{0:T(128)} %copy-done.13) | copy-start | bytes 1540
  439.3 31.1 %copy-start.10 = (f32[128]{0:T(128)S(1)}, f32[128]{0:T(128)}, u32[]{:S(2)}) copy-start(f32[128]{0:T(128)} %copy-done.9) | copy-start | bytes 1540
  469.9 1.7 copy-start.6
  475.2 110.1 %collective-permute-start.6 = (bf16[2,128,512]{1,2,0:T(8,128)(2,1)}, bf16[2,128,512]{1,2,0:T(8,128)(2,1)S(1)}, u32[]{:S(2)}, u32[]{:S(2)}) collective-permute-start(bf16[2,128,512]{1,2,0:T(8,128)(2,1)} %get-tuple-element.143), channel_id=1, source_target_pairs={{0,480},{32,0},{64,32},{96,64},{128,96},{160,128},{192,160},{224,1... | collective-permute-start | bytes 786440 | tf_op jit(solution)/shard_map/ppermute | solution.py:13
  477.2 108.2 %collective-permute-start.7 = (bf16[2,128,512]{1,2,0:T(8,128)(2,1)}, bf16[2,128,512]{1,2,0:T(8,128)(2,1)S(1)}, u32[]{:S(2)}, u32[]{:S(2)}) collective-permute-start(bf16[2,128,512]{1,2,0:T(8,128)(2,1)} %get-tuple-element.144), channel_id=1, source_target_pairs={{0,448},{32,480},{64,0},{96,32},{128,64},{160,96},{192,128},{224,1... | collective-permute-start | bytes 786440 | tf_op jit(solution)/shard_map/ppermute | solution.py:13
  479.1 106.3 %collective-permute-start.9 = (bf16[2,128,512]{1,2,0:T(8,128)(2,1)S(1)}, bf16[2,128,512]{1,2,0:T(8,128)(2,1)S(1)}, u32[]{:S(2)}, u32[]{:S(2)}) collective-permute-start(bf16[2,128,512]{1,2,0:T(8,128)(2,1)S(1)} %get-tuple-element.145), channel_id=1, source_target_pairs={{0,384},{32,416},{64,448},{96,480},{128,0},{160,32},{192,64},{224,... | collective-permute-start | bytes 786440 | tf_op jit(solution)/shard_map/ppermute | solution.py:13
  481.0 104.4 %collective-permute-start.8 = (bf16[2,128,512]{1,2,0:T(8,128)(2,1)S(1)}, bf16[2,128,512]{1,2,0:T(8,128)(2,1)}, u32[]{:S(2)}, u32[]{:S(2)}) collective-permute-start(bf16[2,128,512]{1,2,0:T(8,128)(2,1)S(1)} %get-tuple-element.146), channel_id=1, source_target_pairs={{0,416},{32,448},{64,480},{96,0},{128,32},{160,64},{192,96},{224,1... | collective-permute-start | bytes 786440 | tf_op jit(solution)/shard_map/ppermute | solution.py:13
where the time goes:
time: 589 us; the launch traced here: 588 us
  waiting for transfers between devices  222 us (38%)
  starting transfers between devices  202 us (34%)
  blocking collectives  101 us (17%)
  other arithmetic  51.4 us (9%)
  matrix products  6.17 us (1%)
    ppermute x40, waiting for transfers between devices, passed_along(): lax.ppermute(array, axis, [(i, (i + by) % length) for i in range(length)])  222 us
    ppermute x40, starting transfers between devices, passed_along(): lax.ppermute(array, axis, [(i, (i + by) % length) for i in range(length)])  202 us
    psum x1, blocking collectives, local(): residues_adjoint = lax.psum(jnp.sum(products, axis=0), 'ctx')  101 us
    another operation x1, other arithmetic, forward_step(): jnp.cumsum(growth * segment[:, None, :], axis=0)  29.8 us
  transfers between devices with their start and end apart: 40, of which 36 were waited for; matrix products, arithmetic and copies ran while one was open for 3% of the time, Pallas kernels for 0%

commit v1 on v0

--- a/solution.py
+++ b/solution.py
@@ -156,7 +156,9 @@
     gate_adjoint = (cotangent.astype(jnp.float32) * mixed_rows.reshape(tok_rows, channels)).astype(
         jnp.bfloat16
     )
-    residues_adjoint = lax.psum(jnp.sum(products, axis=0), "ctx")
+    x = jnp.sum(products, axis=0)
+    parts = lax.all_gather(x, "ctx", axis=0, tiled=False)
+    residues_adjoint = parts.sum(axis=0)
     return (queries_adjoint, keys_adjoint, values_adjoint, gate_adjoint, residues_adjoint)
 
 

time: 589 us -> 542 us (0.920)
  the two profiles are of different devices: /device:TPU:30 before, /device:TPU:1 now
where the time goes in v1:
time: 542 us; the launch traced here: 541 us
  starting transfers between devices  233 us (43%)
  waiting for transfers between devices  203 us (37%)
  other arithmetic  51.9 us (10%)
  blocking collectives  41.6 us (8%)
  matrix products  6.14 us (1%)
    ppermute x40, starting transfers between devices, passed_along(): lax.ppermute(array, axis, [(i, (i + by) % length) for i in range(length)])  233 us
    ppermute x40, waiting for transfers between devices, passed_along(): lax.ppermute(array, axis, [(i, (i + by) % length) for i in range(length)])  203 us
    all_gather x1, blocking collectives, local(): parts = lax.all_gather(x, 'ctx', axis=0, tiled=False)  41.6 us
    another operation x1, other arithmetic, forward_step(): jnp.cumsum(growth * segment[:, None, :], axis=0)  29.8 us
    another operation x1, other arithmetic, backward_step(): lax.cumsum(start_weights * segment[:, None, :], axis=0, reverse=True)  11.1 us
  transfers between devices with their start and end apart: 40, of which 35 were waited for; matrix products, arithmetic and copies ran while one was open for 3% of the time, Pallas kernels for 0%

profile of v1, /device:TPU:1, one launch (start us, length us, event | category | flops | bytes accessed | tf_op | source)
XLA Modules:
  0.0 540.7 jit_solution(16508584409205461974)
XLA Ops:
  1.7 4.9 collective-permute-start.2
  8.5 11.1 %fusion.2 = f32[128,16,512]{2,1,0:T(8,128)} fusion(f32[128,512]{1,0:T(8,128)S(1)} %get-tuple-element.156, f32[16,512]{1,0:T(8,128)S(1)} %get-tuple-element.168), kind=kOutput, calls=%fused_computation.10 | output fusion | flops 135266304 | bytes 4489216 | tf_op jit(solution)/shard_map/while/body/eval_jaxpr/reduce_window_sum | solution.py:53
  22.1 4.3 collective-permute-done.3
  26.4 2.8 collective-permute-start.4
  29.7 10.9 %collective-permute-done.4 = bf16[2,128,512]{2,1,0:T(8,128)(2,1)S(1)} collective-permute-done((bf16[2,128,512]{2,1,0:T(8,128)(2,1)S(1)}, bf16[2,128,512]{2,1,0:T(8,128)(2,1)S(1)}, u32[]{:S(2)}, u32[]{:S(2)}) %collective-permute-start.4) | collective-permute-done | bytes 262176 | tf_op jit(solution)/shard_map/ppermute | solution.py:13
  40.7 2.1 collective-permute-start.5
  42.8 12.1 %collective-permute-done.5 = bf16[2,128,512]{2,1,0:T(8,128)(2,1)S(1)} collective-permute-done((bf16[2,128,512]{2,1,0:T(8,128)(2,1)S(1)}, bf16[2,128,512]{2,1,0:T(8,128)(2,1)S(1)}, u32[]{:S(2)}, u32[]{:S(2)}) %collective-permute-start.5) | collective-permute-done | bytes 262176 | tf_op jit(solution)/shard_map/ppermute | solution.py:13
  60.8 191.8 %while.5 = (s32[]{:T(128)}, f32[16,512]{1,0:T(8,128)S(1)}, f32[16,512]{1,0:T(8,128)S(1)}, f32[16,512]{1,0:T(8,128)S(1)}, s32[]{:T(128)}) while((s32[]{:T(128)}, f32[16,512]{1,0:T(8,128)S(1)}, f32[16,512]{1,0:T(8,128)S(1)}, f32[16,512]{1,0:T(8,128)S(1)}, s32[]{:T(128)}) %tuple.71), condition=%wide.region_18.19_spmd, body=%wide.region_17.18_spmd.sunk | while | flops 16386 | bytes 262245 | solution.py:142
  60.8 1.9 collective-permute-start.1
  62.8 12.0 %collective-permute-done.1 = f32[16,512]{1,0:T(8,128)S(1)} collective-permute-done((f32[16,512]{1,0:T(8,128)S(1)}, f32[16,512]{1,0:T(8,128)S(1)}, u32[]{:S(2)}, u32[]{:S(2)}) %collective-permute-start.1) | collective-permute-done | bytes 32800 | tf_op jit(solution)/shard_map/while/body/eval_jaxpr/ppermute | solution.py:13
  74.8 1.9 collective-permute-start.1
  76.7 9.9 %collective-permute-done.1 = f32[16,512]{1,0:T(8,128)S(1)} collective-permute-done((f32[16,512]{1,0:T(8,128)S(1)}, f32[16,512]{1,0:T(8,128)S(1)}, u32[]{:S(2)}, u32[]{:S(2)}) %collective-permute-start.1) | collective-permute-done | bytes 32800 | tf_op jit(solution)/shard_map/while/body/eval_jaxpr/ppermute | solution.py:13
  86.7 1.9 collective-permute-start.1
  88.6 9.9 %collective-permute-done.1 = f32[16,512]{1,0:T(8,128)S(1)} collective-permute-done((f32[16,512]{1,0:T(8,128)S(1)}, f32[16,512]{1,0:T(8,128)S(1)}, u32[]{:S(2)}, u32[]{:S(2)}) %collective-permute-start.1) | collective-permute-done | bytes 32800 | tf_op jit(solution)/shard_map/while/body/eval_jaxpr/ppermute | solution.py:13
  98.5 1.9 collective-permute-start.1
  100.4 9.9 %collective-permute-done.1 = f32[16,512]{1,0:T(8,128)S(1)} collective-permute-done((f32[16,512]{1,0:T(8,128)S(1)}, f32[16,512]{1,0:T(8,128)S(1)}, u32[]{:S(2)}, u32[]{:S(2)}) %collective-permute-start.1) | collective-permute-done | bytes 32800 | tf_op jit(solution)/shard_map/while/body/eval_jaxpr/ppermute | solution.py:13
  110.4 1.9 collective-permute-start.1
  112.3 9.9 %collective-permute-done.1 = f32[16,512]{1,0:T(8,128)S(1)} collective-permute-done((f32[16,512]{1,0:T(8,128)S(1)}, f32[16,512]{1,0:T(8,128)S(1)}, u32[]{:S(2)}, u32[]{:S(2)}) %collective-permute-start.1) | collective-permute-done | bytes 32800 | tf_op jit(solution)/shard_map/while/body/eval_jaxpr/ppermute | solution.py:13
  122.2 1.9 collective-permute-start.1
  124.1 9.9 %collective-permute-done.1 = f32[16,512]{1,0:T(8,128)S(1)} collective-permute-done((f32[16,512]{1,0:T(8,128)S(1)}, f32[16,512]{1,0:T(8,128)S(1)}, u32[]{:S(2)}, u32[]{:S(2)}) %collective-permute-start.1) | collective-permute-done | bytes 32800 | tf_op jit(solution)/shard_map/while/body/eval_jaxpr/ppermute | solution.py:13
  134.1 1.9 collective-permute-start.1
  136.0 9.9 %collective-permute-done.1 = f32[16,512]{1,0:T(8,128)S(1)} collective-permute-done((f32[16,512]{1,0:T(8,128)S(1)}, f32[16,512]{1,0:T(8,128)S(1)}, u32[]{:S(2)}, u32[]{:S(2)}) %collective-permute-start.1) | collective-permute-done | bytes 32800 | tf_op jit(solution)/shard_map/while/body/eval_jaxpr/ppermute | solution.py:13
  145.9 1.9 collective-permute-start.1
  147.8 9.9 %collective-permute-done.1 = f32[16,512]{1,0:T(8,128)S(1)} collective-permute-done((f32[16,512]{1,0:T(8,128)S(1)}, f32[16,512]{1,0:T(8,128)S(1)}, u32[]{:S(2)}, u32[]{:S(2)}) %collective-permute-start.1) | collective-permute-done | bytes 32800 | tf_op jit(solution)/shard_map/while/body/eval_jaxpr/ppermute | solution.py:13
  157.8 1.9 collective-permute-start.1
  159.7 9.9 %collective-permute-done.1 = f32[16,512]{1,0:T(8,128)S(1)} collective-permute-done((f32[16,512]{1,0:T(8,128)S(1)}, f32[16,512]{1,0:T(8,128)S(1)}, u32[]{:S(2)}, u32[]{:S(2)}) %collective-permute-start.1) | collective-permute-done | bytes 32800 | tf_op jit(solution)/shard_map/while/body/eval_jaxpr/ppermute | solution.py:13
  169.6 1.9 collective-permute-start.1
  171.5 9.9 %collective-permute-done.1 = f32[16,512]{1,0:T(8,128)S(1)} collective-permute-done((f32[16,512]{1,0:T(8,128)S(1)}, f32[16,512]{1,0:T(8,128)S(1)}, u32[]{:S(2)}, u32[]{:S(2)}) %collective-permute-start.1) | collective-permute-done | bytes 32800 | tf_op jit(solution)/shard_map/while/body/eval_jaxpr/ppermute | solution.py:13
  181.5 1.9 collective-permute-start.1
  183.4 9.9 %collective-permute-done.1 = f32[16,512]{1,0:T(8,128)S(1)} collective-permute-done((f32[16,512]{1,0:T(8,128)S(1)}, f32[16,512]{1,0:T(8,128)S(1)}, u32[]{:S(2)}, u32[]{:S(2)}) %collective-permute-start.1) | collective-permute-done | bytes 32800 | tf_op jit(solution)/shard_map/while/body/eval_jaxpr/ppermute | solution.py:13
  193.3 1.9 collective-permute-start.1
  195.2 9.9 %collective-permute-done.1 = f32[16,512]{1,0:T(8,128)S(1)} collective-permute-done((f32[16,512]{1,0:T(8,128)S(1)}, f32[16,512]{1,0:T(8,128)S(1)}, u32[]{:S(2)}, u32[]{:S(2)}) %collective-permute-start.1) | collective-permute-done | bytes 32800 | tf_op jit(solution)/shard_map/while/body/eval_jaxpr/ppermute | solution.py:13
  205.2 1.9 collective-permute-start.1
  207.1 9.9 %collective-permute-done.1 = f32[16,512]{1,0:T(8,128)S(1)} collective-permute-done((f32[16,512]{1,0:T(8,128)S(1)}, f32[16,512]{1,0:T(8,128)S(1)}, u32[]{:S(2)}, u32[]{:S(2)}) %collective-permute-start.1) | collective-permute-done | bytes 32800 | tf_op jit(solution)/shard_map/while/body/eval_jaxpr/ppermute | solution.py:13
  217.0 1.9 collective-permute-start.1
  219.0 9.9 %collective-permute-done.1 = f32[16,512]{1,0:T(8,128)S(1)} collective-permute-done((f32[16,512]{1,0:T(8,128)S(1)}, f32[16,512]{1,0:T(8,128)S(1)}, u32[]{:S(2)}, u32[]{:S(2)}) %collective-permute-start.1) | collective-permute-done | bytes 32800 | tf_op jit(solution)/shard_map/while/body/eval_jaxpr/ppermute | solution.py:13
  228.9 1.9 collective-permute-start.1
  230.8 9.9 %collective-permute-done.1 = f32[16,512]{1,0:T(8,128)S(1)} collective-permute-done((f32[16,512]{1,0:T(8,128)S(1)}, f32[16,512]{1,0:T(8,128)S(1)}, u32[]{:S(2)}, u32[]{:S(2)}) %collective-permute-start.1) | collective-permute-done | bytes 32800 | tf_op jit(solution)/shard_map/while/body/eval_jaxpr/ppermute | solution.py:13
  240.7 1.9 collective-permute-start.1
  242.7 9.9 %collective-permute-done.1 = f32[16,512]{1,0:T(8,128)S(1)} collective-permute-done((f32[16,512]{1,0:T(8,128)S(1)}, f32[16,512]{1,0:T(8,128)S(1)}, u32[]{:S(2)}, u32[]{:S(2)}) %collective-permute-start.1) | collective-permute-done | bytes 32800 | tf_op jit(solution)/shard_map/while/body/eval_jaxpr/ppermute | solution.py:13
  252.6 181.4 %while.4 = (s32[]{:T(128)}, f32[16,512]{1,0:T(8,128)S(1)}, f32[16,512]{1,0:T(8,128)S(1)}, f32[16,512]{1,0:T(8,128)S(1)}, s32[]{:T(128)}) while((s32[]{:T(128)}, f32[16,512]{1,0:T(8,128)S(1)}, f32[16,512]{1,0:T(8,128)S(1)}, f32[16,512]{1,0:T(8,128)S(1)}, s32[]{:T(128)}) %tuple.74), condition=%wide.region_4.0_spmd, body=%wide.region_3.4_spmd.sunk | while | flops 16386 | bytes 262245 | solution.py:50
  252.6 11.1 %collective-permute-start = (f32[16,512]{1,0:T(8,128)S(1)}, f32[16,512]{1,0:T(8,128)S(1)}, u32[]{:S(2)}, u32[]{:S(2)}) collective-permute-start(f32[16,512]{1,0:T(8,128)S(1)} %multiply_add_fusion.5), channel_id=1, source_target_pairs={{0,480},{32,0},{64,32},{96,64},{128,96},{160,128},{192,160},{224,1... | collective-permute-start | bytes 98312 | tf_op jit(solution)/shard_map/while/body/eval_jaxpr/ppermute | solution.py:13
  264.6 2.7 collective-permute-start
  267.3 2.6 collective-permute-done
  269.8 9.3 %collective-permute-start = (f32[16,512]{1,0:T(8,128)S(1)}, f32[16,512]{1,0:T(8,128)S(1)}, u32[]{:S(2)}, u32[]{:S(2)}) collective-permute-start(f32[16,512]{1,0:T(8,128)S(1)} %multiply_add_fusion.5), channel_id=1, source_target_pairs={{0,480},{32,0},{64,32},{96,64},{128,96},{160,128},{192,160},{224,1... | collective-permute-start | bytes 98312 | tf_op jit(solution)/shard_map/while/body/eval_jaxpr/ppermute | solution.py:13
  279.9 11.0 %collective-permute-start = (f32[16,512]{1,0:T(8,128)S(1)}, f32[16,512]{1,0:T(8,128)S(1)}, u32[]{:S(2)}, u32[]{:S(2)}) collective-permute-start(f32[16,512]{1,0:T(8,128)S(1)} %multiply_add_fusion.5), channel_id=1, source_target_pairs={{0,480},{32,0},{64,32},{96,64},{128,96},{160,128},{192,160},{224,1... | collective-permute-start | bytes 98312 | tf_op jit(solution)/shard_map/while/body/eval_jaxpr/ppermute | solution.py:13
  291.8 11.0 %collective-permute-start = (f32[16,512]{1,0:T(8,128)S(1)}, f32[16,512]{1,0:T(8,128)S(1)}, u32[]{:S(2)}, u32[]{:S(2)}) collective-permute-start(f32[16,512]{1,0:T(8,128)S(1)} %multiply_add_fusion.5), channel_id=1, source_target_pairs={{0,480},{32,0},{64,32},{96,64},{128,96},{160,128},{192,160},{224,1... | collective-permute-start | bytes 98312 | tf_op jit(solution)/shard_map/while/body/eval_jaxpr/ppermute | solution.py:13
  303.6 11.0 %collective-permute-start = (f32[16,512]{1,0:T(8,128)S(1)}, f32[16,512]{1,0:T(8,128)S(1)}, u32[]{:S(2)}, u32[]{:S(2)}) collective-permute-start(f32[16,512]{1,0:T(8,128)S(1)} %multiply_add_fusion.5), channel_id=1, source_target_pairs={{0,480},{32,0},{64,32},{96,64},{128,96},{160,128},{192,160},{224,1... | collective-permute-start | bytes 98312 | tf_op jit(solution)/shard_map/while/body/eval_jaxpr/ppermute | solution.py:13
  315.5 11.0 %collective-permute-start = (f32[16,512]{1,0:T(8,128)S(1)}, f32[16,512]{1,0:T(8,128)S(1)}, u32[]{:S(2)}, u32[]{:S(2)}) collective-permute-start(f32[16,512]{1,0:T(8,128)S(1)} %multiply_add_fusion.5), channel_id=1, source_target_pairs={{0,480},{32,0},{64,32},{96,64},{128,96},{160,128},{192,160},{224,1... | collective-permute-start | bytes 98312 | tf_op jit(solution)/shard_map/while/body/eval_jaxpr/ppermute | solution.py:13
  327.3 11.0 %collective-permute-start = (f32[16,512]{1,0:T(8,128)S(1)}, f32[16,512]{1,0:T(8,128)S(1)}, u32[]{:S(2)}, u32[]{:S(2)}) collective-permute-start(f32[16,512]{1,0:T(8,128)S(1)} %multiply_add_fusion.5), channel_id=1, source_target_pairs={{0,480},{32,0},{64,32},{96,64},{128,96},{160,128},{192,160},{224,1... | collective-permute-start | bytes 98312 | tf_op jit(solution)/shard_map/while/body/eval_jaxpr/ppermute | solution.py:13
  339.2 11.0 %collective-permute-start = (f32[16,512]{1,0:T(8,128)S(1)}, f32[16,512]{1,0:T(8,128)S(1)}, u32[]{:S(2)}, u32[]{:S(2)}) collective-permute-start(f32[16,512]{1,0:T(8,128)S(1)} %multiply_add_fusion.5), channel_id=1, source_target_pairs={{0,480},{32,0},{64,32},{96,64},{128,96},{160,128},{192,160},{224,1... | collective-permute-start | bytes 98312 | tf_op jit(solution)/shard_map/while/body/eval_jaxpr/ppermute | solution.py:13
  351.1 11.0 %collective-permute-start = (f32[16,512]{1,0:T(8,128)S(1)}, f32[16,512]{1,0:T(8,128)S(1)}, u32[]{:S(2)}, u32[]{:S(2)}) collective-permute-start(f32[16,512]{1,0:T(8,128)S(1)} %multiply_add_fusion.5), channel_id=1, source_target_pairs={{0,480},{32,0},{64,32},{96,64},{128,96},{160,128},{192,160},{224,1... | collective-permute-start | bytes 98312 | tf_op jit(solution)/shard_map/while/body/eval_jaxpr/ppermute | solution.py:13
  362.9 11.0 %collective-permute-start = (f32[16,512]{1,0:T(8,128)S(1)}, f32[16,512]{1,0:T(8,128)S(1)}, u32[]{:S(2)}, u32[]{:S(2)}) collective-permute-start(f32[16,512]{1,0:T(8,128)S(1)} %multiply_add_fusion.5), channel_id=1, source_target_pairs={{0,480},{32,0},{64,32},{96,64},{128,96},{160,128},{192,160},{224,1... | collective-permute-start | bytes 98312 | tf_op jit(solution)/shard_map/while/body/eval_jaxpr/ppermute | solution.py:13
  374.8 11.0 %collective-permute-start = (f32[16,512]{1,0:T(8,128)S(1)}, f32[16,512]{1,0:T(8,128)S(1)}, u32[]{:S(2)}, u32[]{:S(2)}) collective-permute-start(f32[16,512]{1,0:T(8,128)S(1)} %multiply_add_fusion.5), channel_id=1, source_target_pairs={{0,480},{32,0},{64,32},{96,64},{128,96},{160,128},{192,160},{224,1... | collective-permute-start | bytes 98312 | tf_op jit(solution)/shard_map/while/body/eval_jaxpr/ppermute | solution.py:13
  386.6 11.0 %collective-permute-start = (f32[16,512]{1,0:T(8,128)S(1)}, f32[16,512]{1,0:T(8,128)S(1)}, u32[]{:S(2)}, u32[]{:S(2)}) collective-permute-start(f32[16,512]{1,0:T(8,128)S(1)} %multiply_add_fusion.5), channel_id=1, source_target_pairs={{0,480},{32,0},{64,32},{96,64},{128,96},{160,128},{192,160},{224,1... | collective-permute-start | bytes 98312 | tf_op jit(solution)/shard_map/while/body/eval_jaxpr/ppermute | solution.py:13
  398.5 11.0 %collective-permute-start = (f32[16,512]{1,0:T(8,128)S(1)}, f32[16,512]{1,0:T(8,128)S(1)}, u32[]{:S(2)}, u32[]{:S(2)}) collective-permute-start(f32[16,512]{1,0:T(8,128)S(1)} %multiply_add_fusion.5), channel_id=1, source_target_pairs={{0,480},{32,0},{64,32},{96,64},{128,96},{160,128},{192,160},{224,1... | collective-permute-start | bytes 98312 | tf_op jit(solution)/shard_map/while/body/eval_jaxpr/ppermute | solution.py:13
  410.3 11.0 %collective-permute-start = (f32[16,512]{1,0:T(8,128)S(1)}, f32[16,512]{1,0:T(8,128)S(1)}, u32[]{:S(2)}, u32[]{:S(2)}) collective-permute-start(f32[16,512]{1,0:T(8,128)S(1)} %multiply_add_fusion.5), channel_id=1, source_target_pairs={{0,480},{32,0},{64,32},{96,64},{128,96},{160,128},{192,160},{224,1... | collective-permute-start | bytes 98312 | tf_op jit(solution)/shard_map/while/body/eval_jaxpr/ppermute | solution.py:13
  422.2 11.0 %collective-permute-start = (f32[16,512]{1,0:T(8,128)S(1)}, f32[16,512]{1,0:T(8,128)S(1)}, u32[]{:S(2)}, u32[]{:S(2)}) collective-permute-start(f32[16,512]{1,0:T(8,128)S(1)} %multiply_add_fusion.5), channel_id=1, source_target_pairs={{0,480},{32,0},{64,32},{96,64},{128,96},{160,128},{192,160},{224,1... | collective-permute-start | bytes 98312 | tf_op jit(solution)/shard_map/while/body/eval_jaxpr/ppermute | solution.py:13
  434.1 29.8 %multiply_reduce_fusion.2 = (f32[16,512]{1,0:T(8,128)S(1)}, f32[128,512]{1,0:T(8,128)S(1)}, f32[128,512]{1,0:T(8,128)S(1)}) fusion(f32[16,512]{1,0:T(8,128)S(1)} %get-tuple-element.165, f32[128,512]{1,0:T(8,128)S(1)} %get-tuple-element.156, f32[16,512]{1,0:T(8,128)S(1)} %get-tuple-element.164, f32[16,512]{1,0:T(8,128)S(1)} %get-tuple-element.162, ...), kind=kOutput, calls=%fused_computation.4 | output fusion | flops 152952832 | bytes 5473280 | tf_op jit(solution)/shard_map/while/body/eval_jaxpr/jit(cumsum)/reduce_window_sum | solution.py:147
  470.2 11.0 %collective-permute-start.6 = (bf16[2,128,512]{1,2,0:T(8,128)(2,1)}, bf16[2,128,512]{1,2,0:T(8,128)(2,1)S(1)}, u32[]{:S(2)}, u32[]{:S(2)}) collective-permute-start(bf16[2,128,512]{1,2,0:T(8,128)(2,1)} %get-tuple-element.148), channel_id=1, source_target_pairs={{0,480},{32,0},{64,32},{96,64},{128,96},{160,128},{192,160},{224,1... | collective-permute-start | bytes 786440 | tf_op jit(solution)/shard_map/ppermute | solution.py:13
  481.2 9.9 %collective-permute-start.7 = (bf16[2,128,512]{1,2,0:T(8,128)(2,1)S(1)}, bf16[2,128,512]{1,2,0:T(8,128)(2,1)S(1)}, u32[]{:S(2)}, u32[]{:S(2)}) collective-permute-start(bf16[2,128,512]{1,2,0:T(8,128)(2,1)S(1)} %get-tuple-element.149), channel_id=1, source_target_pairs={{0,448},{32,480},{64,0},{96,32},{128,64},{160,96},{192,128},{224,1... | collective-permute-start | bytes 786440 | tf_op jit(solution)/shard_map/ppermute | solution.py:13
  491.0 1.9 collective-permute-start.8
  493.0 1.9 collective-permute-start.9
  495.7 41.6 %all-gather = f32[256,512]{1,0:T(8,128)S(1)} all-gather(f32[16,512]{1,0:T(8,128)S(1)} %get-tuple-element.127), channel_id=2, replica_groups=mesh['ctx'=16,'head'=8,'dp'=4] {'ctx'}, dimensions={0}, use_global_device_ids=true | all-gather | bytes 557056 | tf_op jit(solution)/shard_map/all_gather | solution.py:160
  (151 shorter events, 34.8 us)
Async XLA Ops:
  0.6 21.4 %copy-start.3 = (bf16[128,512]{1,0:T(8,128)(2,1)S(1)}, bf16[128,512]{1,0:T(8,128)(2,1)}, u32[]{:S(2)}) copy-start(bf16[128,512]{1,0:T(8,128)(2,1)} %param.13) | copy-start | bytes 393220
  0.6 21.4 %copy-start.2 = (bf16[128,512]{1,0:T(8,128)(2,1)S(1)}, bf16[128,512]{1,0:T(8,128)(2,1)}, u32[]{:S(2)}) copy-start(bf16[128,512]{1,0:T(8,128)(2,1)} %param.14) | copy-start | bytes 393220
  1.7 17.9 %collective-permute-start.2 = (bf16[2,128,512]{2,1,0:T(8,128)(2,1)S(1)}, bf16[2,128,512]{2,1,0:T(8,128)(2,1)S(1)}, u32[]{:S(2)}, u32[]{:S(2)}) collective-permute-start(bf16[2,128,512]{2,1,0:T(8,128)(2,1)S(1)} %pad_maximum_fusion.1), channel_id=1, source_target_pairs={{0,32},{32,64},{64,96},{96,128},{128,160},{160,192},{192,224},{224... | collective-permute-start | bytes 786440 | tf_op jit(solution)/shard_map/ppermute | solution.py:13
  8.4 46.6 %copy-start.5 = (bf16[128,512]{1,0:T(8,128)(2,1)S(1)}, bf16[128,512]{1,0:T(8,128)(2,1)}, u32[]{:S(2)}) copy-start(bf16[128,512]{1,0:T(8,128)(2,1)} %param.12) | copy-start | bytes 393220
  19.6 6.8 %collective-permute-start.3 = (bf16[2,128,512]{2,1,0:T(8,128)(2,1)S(1)}, bf16[2,128,512]{2,1,0:T(8,128)(2,1)S(1)}, u32[]{:S(2)}, u32[]{:S(2)}) collective-permute-start(bf16[2,128,512]{2,1,0:T(8,128)(2,1)S(1)} %collective-permute-done.2), channel_id=1, source_target_pairs={{0,32},{32,64},{64,96},{96,128},{128,160},{160,192},{192,224},{224... | collective-permute-start | bytes 786440 | tf_op jit(solution)/shard_map/ppermute | solution.py:13
  26.4 14.3 %collective-permute-start.4 = (bf16[2,128,512]{2,1,0:T(8,128)(2,1)S(1)}, bf16[2,128,512]{2,1,0:T(8,128)(2,1)S(1)}, u32[]{:S(2)}, u32[]{:S(2)}) collective-permute-start(bf16[2,128,512]{2,1,0:T(8,128)(2,1)S(1)} %collective-permute-done.3), channel_id=1, source_target_pairs={{0,32},{32,64},{64,96},{96,128},{128,160},{160,192},{192,224},{224... | collective-permute-start | bytes 786440 | tf_op jit(solution)/shard_map/ppermute | solution.py:13
  40.7 14.3 %collective-permute-start.5 = (bf16[2,128,512]{2,1,0:T(8,128)(2,1)S(1)}, bf16[2,128,512]{2,1,0:T(8,128)(2,1)S(1)}, u32[]{:S(2)}, u32[]{:S(2)}) collective-permute-start(bf16[2,128,512]{2,1,0:T(8,128)(2,1)S(1)} %collective-permute-done.4), channel_id=1, source_target_pairs={{0,32},{32,64},{64,96},{96,128},{128,160},{160,192},{192,224},{224... | collective-permute-start | bytes 786440 | tf_op jit(solution)/shard_map/ppermute | solution.py:13
  55.3 2.9 copy-start.9
  56.2 2.8 copy-start.17
  56.3 0.5 copy-start.15
  56.9 0.6 copy-start.13
  57.2 3.6 copy-start.4
  57.6 1.4 copy-start.11
  57.9 376.1 %copy-start.7 = (f32[16,512]{1,0:T(8,128)S(1)}, f32[16,512]{1,0:T(8,128)}, u32[]{:S(2)}) copy-start(f32[16,512]{1,0:T(8,128)} %param.18) | copy-start | bytes 98308
  60.8 14.0 %collective-permute-start.1 = (f32[16,512]{1,0:T(8,128)S(1)}, f32[16,512]{1,0:T(8,128)S(1)}, u32[]{:S(2)}, u32[]{:S(2)}) collective-permute-start(f32[16,512]{1,0:T(8,128)S(1)} %multiply_add_fusion.6), channel_id=1, source_target_pairs={{0,32},{32,64},{64,96},{96,128},{128,160},{160,192},{192,224},{224... | collective-permute-start | bytes 98312 | tf_op jit(solution)/shard_map/while/body/eval_jaxpr/ppermute | solution.py:13
  74.8 11.8 %collective-permute-start.1 = (f32[16,512]{1,0:T(8,128)S(1)}, f32[16,512]{1,0:T(8,128)S(1)}, u32[]{:S(2)}, u32[]{:S(2)}) collective-permute-start(f32[16,512]{1,0:T(8,128)S(1)} %multiply_add_fusion.6), channel_id=1, source_target_pairs={{0,32},{32,64},{64,96},{96,128},{128,160},{160,192},{192,224},{224... | collective-permute-start | bytes 98312 | tf_op jit(solution)/shard_map/while/body/eval_jaxpr/ppermute | solution.py:13
  86.7 11.8 %collective-permute-start.1 = (f32[16,512]{1,0:T(8,128)S(1)}, f32[16,512]{1,0:T(8,128)S(1)}, u32[]{:S(2)}, u32[]{:S(2)}) collective-permute-start(f32[16,512]{1,0:T(8,128)S(1)} %multiply_add_fusion.6), channel_id=1, source_target_pairs={{0,32},{32,64},{64,96},{96,128},{128,160},{160,192},{192,224},{224... | collective-permute-start | bytes 98312 | tf_op jit(solution)/shard_map/while/body/eval_jaxpr/ppermute | solution.py:13
  98.5 11.8 %collective-permute-start.1 = (f32[16,512]{1,0:T(8,128)S(1)}, f32[16,512]{1,0:T(8,128)S(1)}, u32[]{:S(2)}, u32[]{:S(2)}) collective-permute-start(f32[16,512]{1,0:T(8,128)S(1)} %multiply_add_fusion.6), channel_id=1, source_target_pairs={{0,32},{32,64},{64,96},{96,128},{128,160},{160,192},{192,224},{224... | collective-permute-start | bytes 98312 | tf_op jit(solution)/shard_map/while/body/eval_jaxpr/ppermute | solution.py:13
  110.4 11.8 %collective-permute-start.1 = (f32[16,512]{1,0:T(8,128)S(1)}, f32[16,512]{1,0:T(8,128)S(1)}, u32[]{:S(2)}, u32[]{:S(2)}) collective-permute-start(f32[16,512]{1,0:T(8,128)S(1)} %multiply_add_fusion.6), channel_id=1, source_target_pairs={{0,32},{32,64},{64,96},{96,128},{128,160},{160,192},{192,224},{224... | collective-permute-start | bytes 98312 | tf_op jit(solution)/shard_map/while/body/eval_jaxpr/ppermute | solution.py:13
  122.2 11.8 %collective-permute-start.1 = (f32[16,512]{1,0:T(8,128)S(1)}, f32[16,512]{1,0:T(8,128)S(1)}, u32[]{:S(2)}, u32[]{:S(2)}) collective-permute-start(f32[16,512]{1,0:T(8,128)S(1)} %multiply_add_fusion.6), channel_id=1, source_target_pairs={{0,32},{32,64},{64,96},{96,128},{128,160},{160,192},{192,224},{224... | collective-permute-start | bytes 98312 | tf_op jit(solution)/shard_map/while/body/eval_jaxpr/ppermute | solution.py:13
  134.1 11.8 %collective-permute-start.1 = (f32[16,512]{1,0:T(8,128)S(1)}, f32[16,512]{1,0:T(8,128)S(1)}, u32[]{:S(2)}, u32[]{:S(2)}) collective-permute-start(f32[16,512]{1,0:T(8,128)S(1)} %multiply_add_fusion.6), channel_id=1, source_target_pairs={{0,32},{32,64},{64,96},{96,128},{128,160},{160,192},{192,224},{224... | collective-permute-start | bytes 98312 | tf_op jit(solution)/shard_map/while/body/eval_jaxpr/ppermute | solution.py:13
  145.9 11.8 %collective-permute-start.1 = (f32[16,512]{1,0:T(8,128)S(1)}, f32[16,512]{1,0:T(8,128)S(1)}, u32[]{:S(2)}, u32[]{:S(2)}) collective-permute-start(f32[16,512]{1,0:T(8,128)S(1)} %multiply_add_fusion.6), channel_id=1, source_target_pairs={{0,32},{32,64},{64,96},{96,128},{128,160},{160,192},{192,224},{224... | collective-permute-start | bytes 98312 | tf_op jit(solution)/shard_map/while/body/eval_jaxpr/ppermute | solution.py:13
  157.8 11.8 %collective-permute-start.1 = (f32[16,512]{1,0:T(8,128)S(1)}, f32[16,512]{1,0:T(8,128)S(1)}, u32[]{:S(2)}, u32[]{:S(2)}) collective-permute-start(f32[16,512]{1,0:T(8,128)S(1)} %multiply_add_fusion.6), channel_id=1, source_target_pairs={{0,32},{32,64},{64,96},{96,128},{128,160},{160,192},{192,224},{224... | collective-permute-start | bytes 98312 | tf_op jit(solution)/shard_map/while/body/eval_jaxpr/ppermute | solution.py:13
  169.6 11.8 %collective-permute-start.1 = (f32[16,512]{1,0:T(8,128)S(1)}, f32[16,512]{1,0:T(8,128)S(1)}, u32[]{:S(2)}, u32[]{:S(2)}) collective-permute-start(f32[16,512]{1,0:T(8,128)S(1)} %multiply_add_fusion.6), channel_id=1, source_target_pairs={{0,32},{32,64},{64,96},{96,128},{128,160},{160,192},{192,224},{224... | collective-permute-start | bytes 98312 | tf_op jit(solution)/shard_map/while/body/eval_jaxpr/ppermute | solution.py:13
  181.5 11.8 %collective-permute-start.1 = (f32[16,512]{1,0:T(8,128)S(1)}, f32[16,512]{1,0:T(8,128)S(1)}, u32[]{:S(2)}, u32[]{:S(2)}) collective-permute-start(f32[16,512]{1,0:T(8,128)S(1)} %multiply_add_fusion.6), channel_id=1, source_target_pairs={{0,32},{32,64},{64,96},{96,128},{128,160},{160,192},{192,224},{224... | collective-permute-start | bytes 98312 | tf_op jit(solution)/shard_map/while/body/eval_jaxpr/ppermute | solution.py:13
  193.3 11.8 %collective-permute-start.1 = (f32[16,512]{1,0:T(8,128)S(1)}, f32[16,512]{1,0:T(8,128)S(1)}, u32[]{:S(2)}, u32[]{:S(2)}) collective-permute-start(f32[16,512]{1,0:T(8,128)S(1)} %multiply_add_fusion.6), channel_id=1, source_target_pairs={{0,32},{32,64},{64,96},{96,128},{128,160},{160,192},{192,224},{224... | collective-permute-start | bytes 98312 | tf_op jit(solution)/shard_map/while/body/eval_jaxpr/ppermute | solution.py:13
  205.2 11.8 %collective-permute-start.1 = (f32[16,512]{1,0:T(8,128)S(1)}, f32[16,512]{1,0:T(8,128)S(1)}, u32[]{:S(2)}, u32[]{:S(2)}) collective-permute-start(f32[16,512]{1,0:T(8,128)S(1)} %multiply_add_fusion.6), channel_id=1, source_target_pairs={{0,32},{32,64},{64,96},{96,128},{128,160},{160,192},{192,224},{224... | collective-permute-start | bytes 98312 | tf_op jit(solution)/shard_map/while/body/eval_jaxpr/ppermute | solution.py:13
  217.0 11.8 %collective-permute-start.1 = (f32[16,512]{1,0:T(8,128)S(1)}, f32[16,512]{1,0:T(8,128)S(1)}, u32[]{:S(2)}, u32[]{:S(2)}) collective-permute-start(f32[16,512]{1,0:T(8,128)S(1)} %multiply_add_fusion.6), channel_id=1, source_target_pairs={{0,32},{32,64},{64,96},{96,128},{128,160},{160,192},{192,224},{224... | collective-permute-start | bytes 98312 | tf_op jit(solution)/shard_map/while/body/eval_jaxpr/ppermute | solution.py:13
  228.9 11.8 %collective-permute-start.1 = (f32[16,512]{1,0:T(8,128)S(1)}, f32[16,512]{1,0:T(8,128)S(1)}, u32[]{:S(2)}, u32[]{:S(2)}) collective-permute-start(f32[16,512]{1,0:T(8,128)S(1)} %multiply_add_fusion.6), channel_id=1, source_target_pairs={{0,32},{32,64},{64,96},{96,128},{128,160},{160,192},{192,224},{224... | collective-permute-start | bytes 98312 | tf_op jit(solution)/shard_map/while/body/eval_jaxpr/ppermute | solution.py:13
  240.7 11.8 %collective-permute-start.1 = (f32[16,512]{1,0:T(8,128)S(1)}, f32[16,512]{1,0:T(8,128)S(1)}, u32[]{:S(2)}, u32[]{:S(2)}) collective-permute-start(f32[16,512]{1,0:T(8,128)S(1)} %multiply_add_fusion.6), channel_id=1, source_target_pairs={{0,32},{32,64},{64,96},{96,128},{128,160},{160,192},{192,224},{224... | collective-permute-start | bytes 98312 | tf_op jit(solution)/shard_map/while/body/eval_jaxpr/ppermute | solution.py:13
  252.6 12.0 %collective-permute-start = (f32[16,512]{1,0:T(8,128)S(1)}, f32[16,512]{1,0:T(8,128)S(1)}, u32[]{:S(2)}, u32[]{:S(2)}) collective-permute-start(f32[16,512]{1,0:T(8,128)S(1)} %multiply_add_fusion.5), channel_id=1, source_target_pairs={{0,480},{32,0},{64,32},{96,64},{128,96},{160,128},{192,160},{224,1... | collective-permute-start | bytes 98312 | tf_op jit(solution)/shard_map/while/body/eval_jaxpr/ppermute | solution.py:13
  264.6 5.2 collective-permute-start
  269.8 10.1 %collective-permute-start = (f32[16,512]{1,0:T(8,128)S(1)}, f32[16,512]{1,0:T(8,128)S(1)}, u32[]{:S(2)}, u32[]{:S(2)}) collective-permute-start(f32[16,512]{1,0:T(8,128)S(1)} %multiply_add_fusion.5), channel_id=1, source_target_pairs={{0,480},{32,0},{64,32},{96,64},{128,96},{160,128},{192,160},{224,1... | collective-permute-start | bytes 98312 | tf_op jit(solution)/shard_map/while/body/eval_jaxpr/ppermute | solution.py:13
  279.9 11.8 %collective-permute-start = (f32[16,512]{1,0:T(8,128)S(1)}, f32[16,512]{1,0:T(8,128)S(1)}, u32[]{:S(2)}, u32[]{:S(2)}) collective-permute-start(f32[16,512]{1,0:T(8,128)S(1)} %multiply_add_fusion.5), channel_id=1, source_target_pairs={{0,480},{32,0},{64,32},{96,64},{128,96},{160,128},{192,160},{224,1... | collective-permute-start | bytes 98312 | tf_op jit(solution)/shard_map/while/body/eval_jaxpr/ppermute | solution.py:13
  291.8 11.8 %collective-permute-start = (f32[16,512]{1,0:T(8,128)S(1)}, f32[16,512]{1,0:T(8,128)S(1)}, u32[]{:S(2)}, u32[]{:S(2)}) collective-permute-start(f32[16,512]{1,0:T(8,128)S(1)} %multiply_add_fusion.5), channel_id=1, source_target_pairs={{0,480},{32,0},{64,32},{96,64},{128,96},{160,128},{192,160},{224,1... | collective-permute-start | bytes 98312 | tf_op jit(solution)/shard_map/while/body/eval_jaxpr/ppermute | solution.py:13
  303.6 11.8 %collective-permute-start = (f32[16,512]{1,0:T(8,128)S(1)}, f32[16,512]{1,0:T(8,128)S(1)}, u32[]{:S(2)}, u32[]{:S(2)}) collective-permute-start(f32[16,512]{1,0:T(8,128)S(1)} %multiply_add_fusion.5), channel_id=1, source_target_pairs={{0,480},{32,0},{64,32},{96,64},{128,96},{160,128},{192,160},{224,1... | collective-permute-start | bytes 98312 | tf_op jit(solution)/shard_map/while/body/eval_jaxpr/ppermute | solution.py:13
  315.5 11.8 %collective-permute-start = (f32[16,512]{1,0:T(8,128)S(1)}, f32[16,512]{1,0:T(8,128)S(1)}, u32[]{:S(2)}, u32[]{:S(2)}) collective-permute-start(f32[16,512]{1,0:T(8,128)S(1)} %multiply_add_fusion.5), channel_id=1, source_target_pairs={{0,480},{32,0},{64,32},{96,64},{128,96},{160,128},{192,160},{224,1... | collective-permute-start | bytes 98312 | tf_op jit(solution)/shard_map/while/body/eval_jaxpr/ppermute | solution.py:13
  327.3 11.8 %collective-permute-start = (f32[16,512]{1,0:T(8,128)S(1)}, f32[16,512]{1,0:T(8,128)S(1)}, u32[]{:S(2)}, u32[]{:S(2)}) collective-permute-start(f32[16,512]{1,0:T(8,128)S(1)} %multiply_add_fusion.5), channel_id=1, source_target_pairs={{0,480},{32,0},{64,32},{96,64},{128,96},{160,128},{192,160},{224,1... | collective-permute-start | bytes 98312 | tf_op jit(solution)/shard_map/while/body/eval_jaxpr/ppermute | solution.py:13
  339.2 11.8 %collective-permute-start = (f32[16,512]{1,0:T(8,128)S(1)}, f32[16,512]{1,0:T(8,128)S(1)}, u32[]{:S(2)}, u32[]{:S(2)}) collective-permute-start(f32[16,512]{1,0:T(8,128)S(1)} %multiply_add_fusion.5), channel_id=1, source_target_pairs={{0,480},{32,0},{64,32},{96,64},{128,96},{160,128},{192,160},{224,1... | collective-permute-start | bytes 98312 | tf_op jit(solution)/shard_map/while/body/eval_jaxpr/ppermute | solution.py:13
  351.1 11.8 %collective-permute-start = (f32[16,512]{1,0:T(8,128)S(1)}, f32[16,512]{1,0:T(8,128)S(1)}, u32[]{:S(2)}, u32[]{:S(2)}) collective-permute-start(f32[16,512]{1,0:T(8,128)S(1)} %multiply_add_fusion.5), channel_id=1, source_target_pairs={{0,480},{32,0},{64,32},{96,64},{128,96},{160,128},{192,160},{224,1... | collective-permute-start | bytes 98312 | tf_op jit(solution)/shard_map/while/body/eval_jaxpr/ppermute | solution.py:13
  362.9 11.8 %collective-permute-start = (f32[16,512]{1,0:T(8,128)S(1)}, f32[16,512]{1,0:T(8,128)S(1)}, u32[]{:S(2)}, u32[]{:S(2)}) collective-permute-start(f32[16,512]{1,0:T(8,128)S(1)} %multiply_add_fusion.5), channel_id=1, source_target_pairs={{0,480},{32,0},{64,32},{96,64},{128,96},{160,128},{192,160},{224,1... | collective-permute-start | bytes 98312 | tf_op jit(solution)/shard_map/while/body/eval_jaxpr/ppermute | solution.py:13
  374.8 11.8 %collective-permute-start = (f32[16,512]{1,0:T(8,128)S(1)}, f32[16,512]{1,0:T(8,128)S(1)}, u32[]{:S(2)}, u32[]{:S(2)}) collective-permute-start(f32[16,512]{1,0:T(8,128)S(1)} %multiply_add_fusion.5), channel_id=1, source_target_pairs={{0,480},{32,0},{64,32},{96,64},{128,96},{160,128},{192,160},{224,1... | collective-permute-start | bytes 98312 | tf_op jit(solution)/shard_map/while/body/eval_jaxpr/ppermute | solution.py:13
  386.6 11.8 %collective-permute-start = (f32[16,512]{1,0:T(8,128)S(1)}, f32[16,512]{1,0:T(8,128)S(1)}, u32[]{:S(2)}, u32[]{:S(2)}) collective-permute-start(f32[16,512]{1,0:T(8,128)S(1)} %multiply_add_fusion.5), channel_id=1, source_target_pairs={{0,480},{32,0},{64,32},{96,64},{128,96},{160,128},{192,160},{224,1... | collective-permute-start | bytes 98312 | tf_op jit(solution)/shard_map/while/body/eval_jaxpr/ppermute | solution.py:13
  398.5 11.8 %collective-permute-start = (f32[16,512]{1,0:T(8,128)S(1)}, f32[16,512]{1,0:T(8,128)S(1)}, u32[]{:S(2)}, u32[]{:S(2)}) collective-permute-start(f32[16,512]{1,0:T(8,128)S(1)} %multiply_add_fusion.5), channel_id=1, source_target_pairs={{0,480},{32,0},{64,32},{96,64},{128,96},{160,128},{192,160},{224,1... | collective-permute-start | bytes 98312 | tf_op jit(solution)/shard_map/while/body/eval_jaxpr/ppermute | solution.py:13
  410.3 11.8 %collective-permute-start = (f32[16,512]{1,0:T(8,128)S(1)}, f32[16,512]{1,0:T(8,128)S(1)}, u32[]{:S(2)}, u32[]{:S(2)}) collective-permute-start(f32[16,512]{1,0:T(8,128)S(1)} %multiply_add_fusion.5), channel_id=1, source_target_pairs={{0,480},{32,0},{64,32},{96,64},{128,96},{160,128},{192,160},{224,1... | collective-permute-start | bytes 98312 | tf_op jit(solution)/shard_map/while/body/eval_jaxpr/ppermute | solution.py:13
  422.2 11.8 %collective-permute-start = (f32[16,512]{1,0:T(8,128)S(1)}, f32[16,512]{1,0:T(8,128)S(1)}, u32[]{:S(2)}, u32[]{:S(2)}) collective-permute-start(f32[16,512]{1,0:T(8,128)S(1)} %multiply_add_fusion.5), channel_id=1, source_target_pairs={{0,480},{32,0},{64,32},{96,64},{128,96},{160,128},{192,160},{224,1... | collective-permute-start | bytes 98312 | tf_op jit(solution)/shard_map/while/body/eval_jaxpr/ppermute | solution.py:13
  434.0 29.8 %copy-start = (bf16[128,512]{1,0:T(8,128)(2,1)S(1)}, bf16[128,512]{1,0:T(8,128)(2,1)}, u32[]{:S(2)}) copy-start(bf16[128,512]{1,0:T(8,128)(2,1)} %param.16) | copy-start | bytes 393220
  434.1 29.8 %copy-start.1 = (bf16[128,512]{1,0:T(8,128)(2,1)S(1)}, bf16[128,512]{1,0:T(8,128)(2,1)}, u32[]{:S(2)}) copy-start(bf16[128,512]{1,0:T(8,128)(2,1)} %param.15) | copy-start | bytes 393220
  434.1 29.8 %copy-start.8 = (f32[512]{0:T(512)S(1)}, f32[512]{0:T(512)}, u32[]{:S(2)}) copy-start(f32[512]{0:T(512)} %param.19) | copy-start | bytes 6148
  434.1 30.6 %copy-start.10 = (f32[128]{0:T(128)S(1)}, f32[128]{0:T(128)}, u32[]{:S(2)}) copy-start(f32[128]{0:T(128)} %copy-done.9) | copy-start | bytes 1540
  434.1 30.6 %copy-start.16 = (f32[128]{0:T(128)S(1)}, f32[128]{0:T(128)}, u32[]{:S(2)}) copy-start(f32[128]{0:T(128)} %copy-done.15) | copy-start | bytes 1540
  434.1 30.8 %copy-start.14 = (f32[128]{0:T(128)S(1)}, f32[128]{0:T(128)}, u32[]{:S(2)}) copy-start(f32[128]{0:T(128)} %copy-done.13) | copy-start | bytes 1540
  434.1 31.1 %copy-start.12 = (f32[128]{0:T(128)S(1)}, f32[128]{0:T(128)}, u32[]{:S(2)}) copy-start(f32[128]{0:T(128)} %copy-done.11) | copy-start | bytes 1540
  465.4 1.4 copy-start.6
  470.2 67.8 %collective-permute-start.6 = (bf16[2,128,512]{1,2,0:T(8,128)(2,1)}, bf16[2,128,512]{1,2,0:T(8,128)(2,1)S(1)}, u32[]{:S(2)}, u32[]{:S(2)}) collective-permute-start(bf16[2,128,512]{1,2,0:T(8,128)(2,1)} %get-tuple-element.148), channel_id=1, source_target_pairs={{0,480},{32,0},{64,32},{96,64},{128,96},{160,128},{192,160},{224,1... | collective-permute-start | bytes 786440 | tf_op jit(solution)/shard_map/ppermute | solution.py:13
  481.2 56.8 %collective-permute-start.7 = (bf16[2,128,512]{1,2,0:T(8,128)(2,1)S(1)}, bf16[2,128,512]{1,2,0:T(8,128)(2,1)S(1)}, u32[]{:S(2)}, u32[]{:S(2)}) collective-permute-start(bf16[2,128,512]{1,2,0:T(8,128)(2,1)S(1)} %get-tuple-element.149), channel_id=1, source_target_pairs={{0,448},{32,480},{64,0},{96,32},{128,64},{160,96},{192,128},{224,1... | collective-permute-start | bytes 786440 | tf_op jit(solution)/shard_map/ppermute | solution.py:13
  491.0 47.0 %collective-permute-start.8 = (bf16[2,128,512]{1,2,0:T(8,128)(2,1)S(1)}, bf16[2,128,512]{1,2,0:T(8,128)(2,1)S(1)}, u32[]{:S(2)}, u32[]{:S(2)}) collective-permute-start(bf16[2,128,512]{1,2,0:T(8,128)(2,1)S(1)} %get-tuple-element.151), channel_id=1, source_target_pairs={{0,416},{32,448},{64,480},{96,0},{128,32},{160,64},{192,96},{224,1... | collective-permute-start | bytes 786440 | tf_op jit(solution)/shard_map/ppermute | solution.py:13
  493.0 45.0 %collective-permute-start.9 = (bf16[2,128,512]{1,2,0:T(8,128)(2,1)S(1)}, bf16[2,128,512]{1,2,0:T(8,128)(2,1)}, u32[]{:S(2)}, u32[]{:S(2)}) collective-permute-start(bf16[2,128,512]{1,2,0:T(8,128)(2,1)S(1)} %get-tuple-element.150), channel_id=1, source_target_pairs={{0,384},{32,416},{64,448},{96,480},{128,0},{160,32},{192,64},{224,... | collective-permute-start | bytes 786440 | tf_op jit(solution)/shard_map/ppermute | solution.py:13
